TPU v7x, 128 devices: a whole 4x4x4 slice. The times are simulated.
128 devices in a mesh: row: 8 (over y, core), col: 16 (over x, z).
Axes of the slice: x: 4, y: 4, z: 4, core: 2. Of those that a mesh axis runs over, the one named last changes fastest.
Arguments:
- contribution: float32 [8, 8, 4, 16, 128, 128], P(None, 'row', None, 'col'), may hold values from -6 to 6
- parent_tiles: float32 [16, 8, 8, 16, 128, 128], P(None, 'row', None, 'col'), may hold values from -6 to 6
- row_basis: float32 [8, 8, 64, 128], P(None, 'row'), may hold values from -2.4 to 2.4
- pivot_basis: float32 [8, 8, 64, 2048], P(None, 'row', None, 'col'), may hold values from -0.125 to 0.125
- tile_ranks: int32 [64], replicated, may hold values from 16 to 64, as said below
- block_map: int32 [64], replicated, may hold values from 0 to 127, as said below
- panel_start: int32 [1], replicated, may hold values from 0 to 63
- pivot_inverse: float32 [512, 512], replicated
Outputs:
- updated_parent: float32 [16, 8, 8, 16, 128, 128], P(None, 'row', None, 'col')
Inputs may be any that keep to these rules, and one draw needn't show every extreme that they name: `tile_ranks`: multiples of 16; both 16 and 64 occur. `block_map`: child tile row u * 16 + l, for 0 <= l < 16, maps to parent tile row 2 * 16 * u + h_u + l with 0 <= h_u < 16; the 4 values h_u are distinct modulo 8.
All inputs are finite; a program needn't handle non-finite values.
Results may differ from a plain program's by a relative error of at most 0.0003.
Values sent between devices are 32-bit elements; how exact they have to be, the bound alone decides.
No kernel may reach another device: no remote copies, remote signals or barrier semaphores. Data moves between devices by JAX's collectives and lax.ppermute only.
A program may use at most 128 MiB of HBM per device.

v0:
```python
import jax
import jax.numpy as jnp
from jax import lax
from jax.sharding import PartitionSpec as P

PANEL_T = 4


highest = lax.Precision.HIGHEST


def spread_2(x, axis, root):
    mine = lax.axis_index(axis) == root
    return lax.psum(jnp.where(mine, x, jnp.zeros_like(x)), axis)


def from_behind(x, axis, by):
    count = lax.axis_size(axis)
    return lax.ppermute(x, axis, [(i, (i + by) % count) for i in range(count)])


def select_entries(lookup, wanted):
    matches = wanted[:, None] == jnp.arange(lookup.shape[0], dtype=jnp.int32)[None, :]
    return jnp.sum(jnp.where(matches, lookup[None, :], 0), axis=1)


def keep_ranks(factor, tile_index, rank_table):
    limits = select_entries(rank_table, tile_index)
    kept_cols = (jnp.arange(factor.shape[1], dtype=jnp.int32)[None, :] < limits[:, None]).astype(
        jnp.float32
    )
    return factor * kept_cols[:, :, None]


def every_other(stacked, groups, offset):
    shaped = stacked.reshape((groups, stacked.shape[0] // groups) + stacked.shape[1:])
    return lax.dynamic_index_in_dim(shaped, offset, axis=1, keepdims=False)


def per_device(
    contribution,
    parent_tiles,
    row_basis,
    pivot_basis,
    tile_ranks,
    block_map,
    panel_start,
    pivot_inverse,
):
    rows_grid = lax.axis_size("row")
    cols_grid = lax.axis_size("col")
    my_row = lax.axis_index("row")
    my_col = lax.axis_index("col")
    local_rows = contribution.shape[0]
    local_cols = contribution.shape[2]
    parent_rows = parent_tiles.shape[0]
    parent_cols = parent_tiles.shape[2]
    rank_max = row_basis.shape[2]
    per_block = cols_grid // rows_grid
    row_index = jnp.arange(local_rows, dtype=jnp.int32) * rows_grid + my_row
    col_index = jnp.arange(local_cols, dtype=jnp.int32) * cols_grid + my_col
    root_row = my_col % rows_grid
    offset = my_col // rows_grid
    own_basis = keep_ranks(row_basis[:, 0], row_index, tile_ranks)
    own_pivots = pivot_basis[:, 0]
    basis_picked = every_other(row_basis[:, 0], local_cols, offset)
    col_basis = spread_2(basis_picked, "row", root_row)
    all_pivots = lax.all_gather(pivot_basis, "row", axis=1, tiled=True)
    pivot_width = pivot_basis.shape[3]
    grouped = all_pivots.reshape(local_cols, cols_grid, rank_max, pivot_width)
    products = jnp.einsum(
        "trp,scup->cstru",
        own_pivots,
        grouped,
        precision=highest,
        preferred_element_type=jnp.float32,
    )
    weights = lax.psum_scatter(
        products.reshape(lax.axis_size("col") * local_cols, local_rows, rank_max * rank_max),
        "col",
        scatter_dimension=0,
        tiled=True,
    )
    weights = weights.reshape(local_cols, local_rows, rank_max, rank_max)
    col_basis = keep_ranks(col_basis, col_index, tile_ranks)
    half_product = jnp.einsum(
        "trx,stru->tsux", own_basis, weights, precision=highest, preferred_element_type=jnp.float32
    )
    update = jnp.einsum(
        "tsux,suy->tsxy",
        half_product,
        col_basis,
        precision=highest,
        preferred_element_type=jnp.float32,
    )
    lower_mask = (row_index[:, None] >= col_index[None, :])[:, :, None, None]
    payload = jnp.where(lower_mask, contribution[:, 0, :, 0] - update, jnp.float32(0.0))
    block_first = jnp.arange(local_cols, dtype=jnp.int32) * cols_grid
    shifts = select_entries(block_map, block_first) - 2 * block_first
    row_shift = jnp.repeat(shifts, per_block) % rows_grid
    for bit_index in range((rows_grid - 1).bit_length()):
        arrived = from_behind(payload, "row", 1 << bit_index)
        taken = row_shift // (1 << bit_index) % 2 == 1
        payload = jnp.where(taken[:, None, None, None], arrived, payload)
    for bit_index in range((cols_grid - 1).bit_length()):
        arrived = from_behind(payload, "col", 1 << bit_index)
        taken = shifts // (1 << bit_index) % 2 == 1
        payload = jnp.where(taken[None, :, None, None], arrived, payload)
    row_source = (my_row - row_shift) % rows_grid
    target_rows = (
        select_entries(block_map, jnp.arange(local_rows, dtype=jnp.int32) * rows_grid + row_source)
        // rows_grid
    )
    col_source = (my_col - shifts) % cols_grid
    target_cols = (
        select_entries(block_map, jnp.arange(local_cols, dtype=jnp.int32) * cols_grid + col_source)
        // cols_grid
    )
    row_place = (jnp.arange(parent_rows, dtype=jnp.int32)[:, None] == target_rows[None, :]).astype(
        jnp.float32
    )
    col_place = (jnp.arange(parent_cols, dtype=jnp.int32)[:, None] == target_cols[None, :]).astype(
        jnp.float32
    )
    spread = jnp.einsum(
        "at,tsxy->asxy", row_place, payload, precision=highest, preferred_element_type=jnp.float32
    )
    spread = jnp.einsum(
        "bs,asxy->abxy", col_place, spread, precision=highest, preferred_element_type=jnp.float32
    )
    assembled = parent_tiles[:, 0, :, 0] + spread
    start_col = panel_start[0]
    panel_parts = []
    for panel_index in range(PANEL_T):
        column_id = start_col + panel_index
        column = lax.dynamic_index_in_dim(assembled, column_id // cols_grid, axis=1, keepdims=False)
        panel_parts.append(spread_2(column, "col", column_id % cols_grid))
    row_panel = jnp.concatenate(panel_parts, axis=2)
    col_panel = spread_2(every_other(row_panel, parent_cols, offset), "row", root_row)
    scaled = jnp.einsum(
        "axp,pq->axq",
        row_panel,
        pivot_inverse,
        precision=highest,
        preferred_element_type=jnp.float32,
    )
    trailing = jnp.einsum(
        "axq,byq->abxy", scaled, col_panel, precision=highest, preferred_element_type=jnp.float32
    )
    big_rows = jnp.arange(parent_rows, dtype=jnp.int32) * rows_grid + my_row
    big_cols = jnp.arange(parent_cols, dtype=jnp.int32) * cols_grid + my_col
    window = (big_rows[:, None] >= big_cols[None, :]) & (big_cols[None, :] >= start_col + PANEL_T)
    result = jnp.where(window[:, :, None, None], assembled - trailing, assembled)
    return result[:, None, :, None]


def solution(mesh):
    placed = (
        P(None, "row", None, "col", None, None),
        P(None, "row", None, "col", None, None),
        P(None, "row", None, None),
        P(None, "row", None, "col"),
        P(),
        P(),
        P(),
        P(),
    )
    return jax.shard_map(
        per_device,
        mesh=mesh,
        in_specs=placed,
        out_specs=P(None, "row", None, "col", None, None),
        check_vma=False,
    )
```

profile of v0, /device:TPU:0, one launch (start us, length us, event | category | flops | bytes accessed | tf_op | source)
XLA Modules:
  0.0 810.1 jit_solution(2350074608308215927)
XLA Ops:
  7.3 29.4 %all-gather.2.cloned.1.call-done = f32[8,8,64,128]{3,2,1,0:T(8,128)} async-done(((f32[8,1,64,128]{3,2,1,0:T(8,128)}), f32[8,8,64,128]{3,2,1,0:T(8,128)}) %all-gather.2.cloned.1.call-update) | async-done | bytes 2097168 | tf_op jit(solution)/shard_map/all_gather | solution.py:68
  36.7 17.0 %convolution_bitcast_fusion = f32[16,4,8,64,64]{3,4,2,0,1:T(8,128)} fusion(f32[4,16,64,128,1]{3,2,4,1,0:T(8,128)} %bitcast.109, f32[8,1,64,128]{3,2,1,0:T(8,128)} %param.11), kind=kOutput, calls=%fused_computation.1 | convolution fusion | flops 3221225472 | bytes 10747904 | tf_op jit(solution)/shard_map/trp,scup->cstru/dot_general | solution.py:71
  53.7 17.6 %copy.33 = f32[16,4,8,64,64]{4,3,2,1,0:T(8,128)} copy(f32[16,4,8,64,64]{3,4,2,0,1:T(8,128)} %convolution_bitcast_fusion) | data formatting | bytes 16777216 | tf_op jit(solution)/shard_map/trp,scup->cstru/transpose | solution.py:71
  71.4 14.7 %reshape.468 = f32[64,8,4096]{2,1,0:T(8,128)} reshape(f32[16,4,8,64,64]{4,3,2,1,0:T(8,128)} %copy.33) | data formatting | bytes 16777216 | tf_op jit(solution)/shard_map/reshape | solution.py:79
  90.2 81.2 %reduce-scatter.2.cloned.1.call-done = f32[4,8,4096]{2,1,0:T(8,128)} async-done(((f32[64,8,4096]{2,1,0:T(8,128)}), f32[4,8,4096]{2,1,0:T(8,128)}) %reduce-scatter.2.cloned.1.call-update) | async-done | bytes 524304 | tf_op jit(solution)/shard_map/reduce_scatter | solution.py:78
  175.8 56.6 %all-reduce.5.cloned.1.call-done = f32[4,64,128]{2,1,0:T(8,128)} async-done(((f32[4,64,128]{2,1,0:T(8,128)}), f32[4,64,128]{2,1,0:T(8,128)}) %all-reduce.5.cloned.1.call-update) | async-done | bytes 131088 | tf_op jit(solution)/shard_map/psum | solution.py:14
  232.3 3.9 fusion.9
  236.7 26.3 %collective-permute-done = f32[8,4,128,128]{2,3,0,1:T(8,128)} collective-permute-done((f32[8,4,128,128]{2,3,0,1:T(8,128)S(1)}, f32[8,4,128,128]{2,3,0,1:T(8,128)}, u32[]{:S(2)}, u32[]{:S(2)}) %collective-permute-start) | collective-permute-done | bytes 2097184 | tf_op jit(solution)/shard_map/ppermute | solution.py:19
  265.0 45.3 %collective-permute-done.1 = f32[8,4,128,128]{2,3,0,1:T(8,128)S(1)} collective-permute-done((f32[8,4,128,128]{2,3,0,1:T(8,128)S(1)}, f32[8,4,128,128]{2,3,0,1:T(8,128)S(1)}, u32[]{:S(2)}, u32[]{:S(2)}) %collective-permute-start.1) | collective-permute-done | bytes 2097184 | tf_op jit(solution)/shard_map/ppermute | solution.py:19
  311.6 45.3 %collective-permute-done.2 = f32[8,4,128,128]{2,3,0,1:T(8,128)S(1)} collective-permute-done((f32[8,4,128,128]{2,3,0,1:T(8,128)S(1)}, f32[8,4,128,128]{2,3,0,1:T(8,128)S(1)}, u32[]{:S(2)}, u32[]{:S(2)}) %collective-permute-start.2) | collective-permute-done | bytes 2097184 | tf_op jit(solution)/shard_map/ppermute | solution.py:19
  359.1 47.1 %collective-permute-done.3 = f32[8,4,128,128]{2,3,0,1:T(8,128)S(1)} collective-permute-done((f32[8,4,128,128]{2,3,0,1:T(8,128)S(1)}, f32[8,4,128,128]{2,3,0,1:T(8,128)S(1)}, u32[]{:S(2)}, u32[]{:S(2)}) %collective-permute-start.3) | collective-permute-done | bytes 2097184 | tf_op jit(solution)/shard_map/ppermute | solution.py:19
  406.7 49.8 %collective-permute-done.4 = f32[8,4,128,128]{2,3,0,1:T(8,128)S(1)} collective-permute-done((f32[8,4,128,128]{2,3,0,1:T(8,128)S(1)}, f32[8,4,128,128]{2,3,0,1:T(8,128)S(1)}, u32[]{:S(2)}, u32[]{:S(2)}) %collective-permute-start.4) | collective-permute-done | bytes 2097184 | tf_op jit(solution)/shard_map/ppermute | solution.py:19
  457.0 65.4 %collective-permute-done.5 = f32[8,4,128,128]{2,3,0,1:T(8,128)S(1)} collective-permute-done((f32[8,4,128,128]{2,3,0,1:T(8,128)S(1)}, f32[8,4,128,128]{2,3,0,1:T(8,128)S(1)}, u32[]{:S(2)}, u32[]{:S(2)}) %collective-permute-start.5) | collective-permute-done | bytes 2097184 | tf_op jit(solution)/shard_map/ppermute | solution.py:19
  524.0 26.5 %collective-permute-done.6 = f32[8,4,128,128]{2,3,0,1:T(8,128)} collective-permute-done((f32[8,4,128,128]{2,3,0,1:T(8,128)S(1)}, f32[8,4,128,128]{2,3,0,1:T(8,128)}, u32[]{:S(2)}, u32[]{:S(2)}) %collective-permute-start.6) | collective-permute-done | bytes 2097184 | tf_op jit(solution)/shard_map/ppermute | solution.py:19
  550.4 3.2 broadcast_select_fusion.7
  557.6 13.0 %bitcast_add_fusion = f32[16,8,128,128]{3,1,2,0:T(8,128)S(1)} fusion(f32[16,1,8,1,128,128]{5,4,3,2,1,0:T(8,128)} %param.9, f32[16,4,128,128]{3,0,2,1:T(8,128)S(1)} %fusion.21, s32[4]{0:T(128)S(1)} %and_select_fusion), kind=kOutput, calls=%fused_computation.3 | convolution fusion | flops 102760480 | bytes 20971536 | tf_op jit(solution)/shard_map/bs,asxy->abxy/dot_general | solution.py:128
  571.9 5.8 broadcast_select_fusion
  580.6 104.6 %all-reduce.9.cloned.1.call-done = (f32[16,128,128]{2,1,0:T(8,128)}, f32[16,128,128]{2,1,0:T(8,128)}, f32[16,128,128]{2,1,0:T(8,128)}, f32[16,128,128]{2,1,0:T(8,128)}) async-done(((f32[16,128,128]{2,1,0:T(8,128)}, f32[16,128,128]{2,1,0:T(8,128)}, f32[16,128,128]{2,1,0:T(8,128)}, f32[16,128,128]{2,1,0:T(8,128)}), (f32[16,128,128]{2,1,0:T(8,128)}, f32[16,128,128]{2,1,0:T(8,128)}, f32[16,128,128]{2,1,0:T(8,128)}, ...) | async-done | bytes 4194320 | tf_op jit(solution)/shard_map/psum | solution.py:14
  691.9 9.9 %fusion.10 = f32[16,128,512]{2,1,0:T(8,128)} fusion(f32[16,128,512]{2,1,0:T(8,128)} %copy-done.2, f32[512,512]{1,0:T(8,128)S(1)} %copy-done), kind=kOutput, calls=%fused_computation.14 | convolution fusion | flops 6442450944 | bytes 9437184 | tf_op jit(solution)/shard_map/axp,pq->axq/dot_general | solution.py:140
  701.8 55.5 %all-reduce.7.cloned.1.call-done = f32[8,128,512]{2,1,0:T(8,128)} async-done(((f32[8,128,512]{2,1,0:T(8,128)}), f32[8,128,512]{2,1,0:T(8,128)}) %all-reduce.7.cloned.1.call-update) | async-done | bytes 2097168 | tf_op jit(solution)/shard_map/psum | solution.py:14
  757.3 18.0 %fusion.1 = f32[8,128,16,128]{3,1,2,0:T(8,128)} fusion(f32[16,128,512]{2,1,0:T(8,128)} %fusion.10, f32[8,128,512]{2,1,0:T(8,128)} %all-reduce.7.cloned.1.call-done), kind=kOutput, calls=%fused_computation.4 | convolution fusion | flops 12884901888 | bytes 14680064 | tf_op jit(solution)/shard_map/axq,byq->abxy/dot_general | solution.py:147
  775.3 9.5 %copy.42 = f32[8,128,16,128]{1,0,3,2:T(8,128)} copy(f32[8,128,16,128]{3,1,2,0:T(8,128)} %fusion.1) | data formatting | bytes 16777216 | tf_op jit(solution)/shard_map/axq,byq->abxy/dot_general | solution.py:147
  784.8 10.2 %fusion = f32[16,1,8,1,128,128]{5,2,4,0,3,1:T(8,128)} fusion(f32[16,8,128,128]{3,1,2,0:T(8,128)} %copy-done.1, f32[8,128,16,128]{1,0,3,2:T(8,128)} %copy.42, pred[16,8]{1,0:T(8,128)(4,1)S(1)} %compare_and_fusion), kind=kLoop, calls=%fused_computation.2 | loop fusion | flops 4194304 | bytes 25165952 | tf_op jit(solution)/shard_map/broadcast_in_dim | solution.py:154
  794.9 8.2 %copy.43 = f32[16,1,8,1,128,128]{5,4,3,2,1,0:T(8,128)} copy(f32[16,1,8,1,128,128]{5,2,4,0,3,1:T(8,128)} %fusion) | data formatting | bytes 16777216 | tf_op jit(solution)/shard_map/broadcast_in_dim | solution.py:154
  (80 shorter events, 31.4 us)
Async XLA Ops:
  6.5 685.4 %copy-start = (f32[512,512]{1,0:T(8,128)S(1)}, f32[512,512]{1,0:T(8,128)}, u32[]{:S(2)}) copy-start(f32[512,512]{1,0:T(8,128)} %param.15) | copy-start | bytes 3145732
  6.5 30.2 %all-gather.2.cloned.1.call-start = ((), (), s32[]{:S(2)}) async-start(), calls=%async_computation.2 | async-start | bytes 2359296 | tf_op jit(solution)/shard_map/all_gather | solution.py:68
  7.3 164.2 %reduce-scatter.2.cloned.1.call-start = ((), (), s32[]{:S(2)}) async-start(), calls=%async_computation.3 | async-start | bytes 8912896 | tf_op jit(solution)/shard_map/reduce_scatter | solution.py:78
  86.1 0.9 copy-start.7
  86.1 1.8 copy-start.8
  86.1 2.3 copy-start.3
  86.1 146.2 %all-reduce.5.cloned.1.call-start = ((), (), s32[]{:S(2)}) async-start(), calls=%async_computation.1 | async-start | bytes 262144 | tf_op jit(solution)/shard_map/psum | solution.py:14
  87.7 597.5 %all-reduce.9.cloned.1.call-start = ((), (), s32[]{:S(2)}) async-start(), calls=%async_computation.5 | async-start | bytes 8388608 | tf_op jit(solution)/shard_map/psum | solution.py:14
  175.8 60.5 %copy-start.9 = (s32[64]{0:T(128)S(1)}, s32[64]{0:T(128)}, u32[]{:S(2)}) copy-start(s32[64]{0:T(128)} %param.13) | copy-start | bytes 772
  236.3 26.8 %collective-permute-start = (f32[8,4,128,128]{2,3,0,1:T(8,128)S(1)}, f32[8,4,128,128]{2,3,0,1:T(8,128)}, u32[]{:S(2)}, u32[]{:S(2)}) collective-permute-start(f32[8,4,128,128]{2,3,0,1:T(8,128)S(1)} %fusion.9), channel_id=1, source_target_pairs={{0,16},{16,32},{32,48},{48,64},{64,80},{80,96},{96,112},{112,0},{1... | collective-permute-start | bytes 6291464 | tf_op jit(solution)/shard_map/ppermute | solution.py:19
  264.9 45.4 %collective-permute-start.1 = (f32[8,4,128,128]{2,3,0,1:T(8,128)S(1)}, f32[8,4,128,128]{2,3,0,1:T(8,128)S(1)}, u32[]{:S(2)}, u32[]{:S(2)}) collective-permute-start(f32[8,4,128,128]{2,3,0,1:T(8,128)S(1)} %broadcast_select_fusion.1), channel_id=1, source_target_pairs={{0,32},{16,48},{32,64},{48,80},{64,96},{80,112},{96,0},{112,16},{1... | collective-permute-start | bytes 6291464 | tf_op jit(solution)/shard_map/ppermute | solution.py:19
  310.8 46.1 %collective-permute-start.2 = (f32[8,4,128,128]{2,3,0,1:T(8,128)S(1)}, f32[8,4,128,128]{2,3,0,1:T(8,128)S(1)}, u32[]{:S(2)}, u32[]{:S(2)}) collective-permute-start(f32[8,4,128,128]{2,3,0,1:T(8,128)S(1)} %broadcast_select_fusion.2), channel_id=1, source_target_pairs={{0,64},{16,80},{32,96},{48,112},{64,0},{80,16},{96,32},{112,48},{1... | collective-permute-start | bytes 6291464 | tf_op jit(solution)/shard_map/ppermute | solution.py:19
  357.3 48.9 %collective-permute-start.3 = (f32[8,4,128,128]{2,3,0,1:T(8,128)S(1)}, f32[8,4,128,128]{2,3,0,1:T(8,128)S(1)}, u32[]{:S(2)}, u32[]{:S(2)}) collective-permute-start(f32[8,4,128,128]{2,3,0,1:T(8,128)S(1)} %broadcast_select_fusion.3), channel_id=1, source_target_pairs={{0,1},{1,2},{2,3},{3,4},{4,5},{5,6},{6,7},{7,8},{8,9},{9,10},{10,1... | collective-permute-start | bytes 6291464 | tf_op jit(solution)/shard_map/ppermute | solution.py:19
  406.6 49.9 %collective-permute-start.4 = (f32[8,4,128,128]{2,3,0,1:T(8,128)S(1)}, f32[8,4,128,128]{2,3,0,1:T(8,128)S(1)}, u32[]{:S(2)}, u32[]{:S(2)}) collective-permute-start(f32[8,4,128,128]{2,3,0,1:T(8,128)S(1)} %broadcast_select_fusion.4), channel_id=1, source_target_pairs={{0,2},{1,3},{2,4},{3,5},{4,6},{5,7},{6,8},{7,9},{8,10},{9,11},{10,... | collective-permute-start | bytes 6291464 | tf_op jit(solution)/shard_map/ppermute | solution.py:19
  456.9 65.5 %collective-permute-start.5 = (f32[8,4,128,128]{2,3,0,1:T(8,128)S(1)}, f32[8,4,128,128]{2,3,0,1:T(8,128)S(1)}, u32[]{:S(2)}, u32[]{:S(2)}) collective-permute-start(f32[8,4,128,128]{2,3,0,1:T(8,128)S(1)} %broadcast_select_fusion.5), channel_id=1, source_target_pairs={{0,4},{1,5},{2,6},{3,7},{4,8},{5,9},{6,10},{7,11},{8,12},{9,13},{1... | collective-permute-start | bytes 6291464 | tf_op jit(solution)/shard_map/ppermute | solution.py:19
  522.7 27.7 %collective-permute-start.6 = (f32[8,4,128,128]{2,3,0,1:T(8,128)S(1)}, f32[8,4,128,128]{2,3,0,1:T(8,128)}, u32[]{:S(2)}, u32[]{:S(2)}) collective-permute-start(f32[8,4,128,128]{2,3,0,1:T(8,128)S(1)} %broadcast_select_fusion.6), channel_id=1, source_target_pairs={{0,8},{1,9},{2,10},{3,11},{4,12},{5,13},{6,14},{7,15},{8,0},{9,1},... | collective-permute-start | bytes 6291464 | tf_op jit(solution)/shard_map/ppermute | solution.py:19
  570.6 7.0 copy-start.1
  580.3 177.0 %all-reduce.7.cloned.1.call-start = ((), (), s32[]{:S(2)}) async-start(), calls=%async_computation.4 | async-start | bytes 4194304 | tf_op jit(solution)/shard_map/psum | solution.py:14
  685.3 1.5 copy-start.6
  685.3 1.9 copy-start.5
  686.8 1.3 copy-start.4
  688.2 2.0 copy-start.2
Sparse Core Ops, SparseCore 0:
  9.1 27.6 all-gather.1
  86.2 85.1 reduce-scatter.1
  173.8 58.5 all-reduce.4
  580.5 104.7 all-reduce.8
  691.9 65.3 all-reduce.6
where the time goes:
time: 820 us; the launch traced here: 810 us
  waiting for transfers between devices  634 us (77%)
  matrix products  66.6 us (8%)
  local copies, waits for them, and re-layouts  62.5 us (8%)
  other arithmetic  29.3 us (4%)
  between operations  14.7 us (2%)
    ppermute x7, waiting for transfers between devices, from_behind(): return lax.ppermute(x, axis, [(i, (i + by) % count) for i in range(count)])  306 us
    psum x3, waiting for transfers between devices, spread_2(): return lax.psum(jnp.where(mine, x, jnp.zeros_like(x)), axis)  217 us
    reduce_scatter x1, waiting for transfers between devices, per_device(): lax.psum_scatter(products.reshape(lax.axis_size('col') * local_cols, loca...  81.2 us
    all_gather x1, waiting for transfers between devices, per_device(): all_pivots = lax.all_gather(pivot_basis, 'row', axis=1, tiled=True)  29.4 us
    dot_general x1, matrix products, per_device(): jnp.einsum('axq,byq->abxy', scaled, col_panel, precision=highest, preferr...  18 us
    transpose x1, local copies, waits for them, and re-layouts, per_device(): jnp.einsum('trp,scup->cstru', own_pivots, grouped, precision=highest, pre...  17.6 us
    dot_general x1, matrix products, per_device(): jnp.einsum('trp,scup->cstru', own_pivots, grouped, precision=highest, pre...  17 us
  transfers between devices with their start and end apart: 12, of which 12 were waited for; matrix products, arithmetic and copies ran while one was open for 2% of the time, Pallas kernels for 0%

commit v1 on v0

v1 whole, which is shorter than its diff:
```python
import jax
import jax.numpy as jnp
from jax import lax
from jax.experimental import pallas as pl
from jax.experimental.pallas import tpu as pltpu
from jax.sharding import PartitionSpec as P

PANEL_T = 4
F32 = jnp.float32
BF16 = jnp.bfloat16


def shift_of(meta, u):
    return meta[16 * u] - 32 * u


def chunk_of(meta, rho):
    row = meta[129]
    side = (rho + row) & 1
    return 4 * side + (((row >> 1) - (rho >> 1)) & 3)


def row_source(meta, u):
    return (meta[129] - shift_of(meta, u)) & 7


def col_source(meta, s, col):
    return (col - shift_of(meta, s)) & 15


def split2(x):
    hi = x.astype(BF16)
    return hi, (x - hi.astype(F32)).astype(BF16)


def dot3(a, b, dims):
    dn = (dims, ((), ()))
    ah, al = a
    bh, bl = b
    low = lax.dot_general(ah, bl, dn, preferred_element_type=F32)
    low += lax.dot_general(al, bh, dn, preferred_element_type=F32)
    return lax.dot_general(ah, bh, dn, preferred_element_type=F32) + low


NT = ((1,), (1,))
NN = ((1,), (0,))
TN = ((0,), (0,))


def row_perm(x, dy, dc):
    pairs = [(2 * y + k, 2 * ((y + dy) % 4) + (k + dc) % 2) for y in range(4) for k in range(2)]
    return lax.ppermute(x, "row", pairs)


def col_perm(x, dx, dz):
    pairs = [(4 * a + b, 4 * ((a + dx) % 4) + (b + dz) % 4) for a in range(4) for b in range(4)]
    return lax.ppermute(x, "col", pairs)


def gather_rows(x):
    ring = jnp.stack([x] + [row_perm(x, d, 0) for d in (1, 2, 3)])
    return jnp.concatenate([ring, row_perm(ring, 0, 1)])


def rotate(x, axis, count, by):
    def step(k):
        pairs = [(i, (i + k) % count) for i in range(count)]
        return (lambda v: lax.ppermute(v, axis, pairs)) if k else (lambda v: v)

    return lax.switch(by, [step(k) for k in range(count)], x)


def products_kernel(meta, v_ref, *refs):
    a_refs, b_refs = refs[0:4], refs[4:8]
    hi_ref, lo_ref = refs[8], refs[9]
    for u in range(4):
        own = v_ref[chunk_of(meta, row_source(meta, u)), 2 * u : 2 * u + 2]
        hi, lo = split2(own.reshape(128, 128))
        hi_ref[128 * u : 128 * u + 128] = hi
        lo_ref[128 * u : 128 * u + 128] = lo

    def left(first, last):
        return hi_ref[first:last], lo_ref[first:last]

    def right(col, s, q):
        parts = []
        for k in (s, q):
            j = col_source(meta, k, col)
            parts.append(v_ref[chunk_of(meta, j & 7), 2 * k + (j >> 3)])
        return split2(jnp.concatenate(parts, axis=0))

    col = meta[130]
    x, z = col >> 2, col & 3
    low_half = lax.broadcasted_iota(jnp.int32, (128, 128), 1) < 64
    for d in range(4):

        def upper(e, carry):
            other = 4 * ((x + e) & 3) + ((z + d) & 3)
            a_refs[d][e] = dot3(left(128, 448), right(other, 0, 1), NT)
            return carry

        def lower(e, carry):
            other = 4 * ((x + d) & 3) + ((z + e) & 3)
            b_refs[d][e, 0:64] = dot3(left(448, 512), right(other, 0, 1), NT)
            ends = right(other, 0, 3)
            b_refs[d][e, 64:192] = jnp.where(
                low_half, dot3(left(0, 128), ends, NT), dot3(left(384, 512), ends, NT)
            )
            mid = right(other, 2, 2)
            b_refs[d][e, 192:320] = jnp.where(
                low_half, dot3(left(256, 384), mid, NT), dot3(left(384, 512), mid, NT)
            )
            return carry

        lax.fori_loop(0, 4, upper, 0)
        lax.fori_loop(0, 4, lower, 0)


def products(meta, pivots):
    whole = pl.BlockSpec(memory_space=pltpu.VMEM)
    return pl.pallas_call(
        products_kernel,
        grid_spec=pltpu.PrefetchScalarGridSpec(
            num_scalar_prefetch=1,
            grid=(),
            in_specs=[whole],
            out_specs=[whole] * 8,
            scratch_shapes=[pltpu.VMEM((512, 128), BF16)] * 2,
        ),
        out_shape=[jax.ShapeDtypeStruct((4, 320, 128), F32)] * 8,
        compiler_params=pltpu.CompilerParams(vmem_limit_bytes=24 << 20),
        cost_estimate=pl.CostEstimate(flops=2 * 10**9, bytes_accessed=8 << 20, transcendentals=0),
    )(meta, pivots)


def scatter_sums(parts, first, second):
    arrived = [parts[0]] + [first(parts[d], d) for d in (1, 2, 3)]
    sums = [arrived[0][e] + arrived[1][e] + arrived[2][e] + arrived[3][e] for e in range(4)]
    return [sums[0]] + [second(sums[e], e) for e in (1, 2, 3)]


def moved_kernel(meta, *refs):
    wa, wb = refs[0:4], refs[4:8]
    base_ref, c_refs, parent_ref = refs[8], refs[9:13], refs[13]
    out_ref, pcol_ref = refs[14], refs[15]
    g_ref = refs[16]
    col = meta[130]
    rank_rows = lax.broadcasted_iota(jnp.int32, (64, 128), 0)

    def basis(rho, t, tile):
        return jnp.where(rank_rows < meta[64 + tile], base_ref[chunk_of(meta, rho), t], 0.0)

    def col_basis(s):
        j = col_source(meta, s, col)
        return basis(j & 7, 2 * s + (j >> 3), 16 * s + j)

    bj = [col_basis(s) for s in range(4)]
    zero = jnp.zeros((64, 128), F32)

    def diagonal(s, q):
        top = jnp.concatenate([bj[s], zero], axis=1)
        bottom = jnp.concatenate([zero, bj[q]], axis=1)
        return split2(jnp.concatenate([top, bottom], axis=0))

    d01, d03, d22 = diagonal(0, 1), diagonal(0, 3), diagonal(2, 2)
    a_sum = wa[0][...] + wa[1][...] + wa[2][...] + wa[3][...]
    b_sum = wb[0][...] + wb[1][...] + wb[2][...] + wb[3][...]
    g_ref[0:320] = dot3(split2(a_sum), d01, NN)
    g_ref[320:384] = dot3(split2(b_sum[0:64]), d01, NN)
    g_ref[384:512] = dot3(split2(b_sum[64:192]), d03, NN)
    g_ref[512:640] = dot3(split2(b_sum[192:320]), d22, NN)

    for t in range(8):
        u, w = t // 2, t % 2
        rho = row_source(meta, u)
        bi = split2(basis(rho, t, 16 * u + 8 * w + rho))

        def put(s, tile):
            value = c_refs[s][2 * (u - s) + w] - tile
            if u == s:
                keep = rho + 8 * w >= col_source(meta, s, col)
                value = jnp.where(keep, value, 0.0)
            out_ref[u * (u + 1) + w * (u + 1) + s] = value

        def update(first, lane, wide):
            return dot3(bi, split2(g_ref[first : first + 64, lane : lane + wide]), TN)

        if t >= 2:
            both = update(64 * (t - 2), 0, 256)
            put(0, both[:, 0:128])
            put(1, both[:, 128:256])
        else:
            put(0, update(384 + 64 * t, 0, 128))
        if u == 2:
            put(2, update(512 + 64 * w, 0, 128))
        if u == 3:
            put(2, update(512 + 64 * w, 128, 128))
            put(3, update(384 + 64 * w, 128, 128))

    start = meta[128]
    place = (col - start) & 15
    tile_col = start + place
    b = tile_col >> 4
    s = b >> 1

    def add(a, carry):
        u = a >> 2
        tile_row = 8 * a + meta[129]
        at = tile_row - meta[16 * u]
        at_col = tile_col - meta[16 * s]
        use = (at >= 0) & (at < 16) & (at_col >= 0) & (at_col < 16) & (u >= s)
        index = jnp.where(use, u * (u + 1) + (at >> 3) * (u + 1) + s, 0)
        pcol_ref[a] = parent_ref[a, 0, 0, 0] + jnp.where(use, out_ref[index], 0.0)
        return carry

    lax.fori_loop(0, 16, add, 0)


def panel_block(meta):
    start = meta[128]
    return jnp.minimum((start + ((meta[130] - start) & 15)) >> 4, 7)


def moved_tiles(meta, wa, wb, bases, cols, parent_tiles):
    whole = pl.BlockSpec(memory_space=pltpu.VMEM)
    parent_spec = pl.BlockSpec(
        (16, 1, 1, 1, 128, 128), lambda i, meta: (0, 0, panel_block(meta), 0, 0, 0)
    )
    return pl.pallas_call(
        moved_kernel,
        grid_spec=pltpu.PrefetchScalarGridSpec(
            num_scalar_prefetch=1,
            grid=(1,),
            in_specs=[whole] * 13 + [parent_spec],
            out_specs=[whole, whole],
            scratch_shapes=[pltpu.VMEM((640, 256), F32)],
        ),
        out_shape=[
            jax.ShapeDtypeStruct((20, 128, 128), F32),
            jax.ShapeDtypeStruct((16, 128, 128), F32),
        ],
        compiler_params=pltpu.CompilerParams(vmem_limit_bytes=32 << 20),
        cost_estimate=pl.CostEstimate(flops=10**9, bytes_accessed=8 << 20, transcendentals=0),
    )(meta, *wa, *wb, bases, *cols, parent_tiles)


def scaled_kernel(meta, got_ref, inverse_ref, panel_ref, sa_ref, sb_ref):
    start = meta[128]
    tiles = [got_ref[(start + p) & 15] for p in range(PANEL_T)]
    panel = jnp.concatenate(tiles, axis=1)
    panel_ref[...] = panel
    out = dot3(split2(panel), split2(inverse_ref[...]), NN)
    sa_ref[...] = out[0:64]
    sb_ref[...] = out[64:128]


def scale_panel(meta, got, inverse):
    whole = pl.BlockSpec(memory_space=pltpu.VMEM)
    return pl.pallas_call(
        scaled_kernel,
        grid_spec=pltpu.PrefetchScalarGridSpec(
            num_scalar_prefetch=1, grid=(), in_specs=[whole] * 2, out_specs=[whole] * 3
        ),
        out_shape=[
            jax.ShapeDtypeStruct((128, 512), F32),
            jax.ShapeDtypeStruct((64, 512), F32),
            jax.ShapeDtypeStruct((64, 512), F32),
        ],
        compiler_params=pltpu.CompilerParams(vmem_limit_bytes=24 << 20),
        cost_estimate=pl.CostEstimate(flops=2 * 10**8, bytes_accessed=3 << 20, transcendentals=0),
    )(meta, got, inverse)


def trailing_kernel(
    meta, parent_ref, moved_ref, sa_ref, sb_ref, panel_ref, out_ref, sh_ref, sl_ref, ph_ref, pl_ref
):
    q, g = pl.program_id(0), pl.program_id(1)
    row, col, start = meta[129], meta[130], meta[128]
    x, z = col >> 2, col & 3

    @pl.when(q == 0)
    def _():
        for k in range(4):
            a = 4 * g + k
            e, d = (x - (a >> 2)) & 3, (z - (a & 3)) & 3
            hi, lo = split2(sa_ref[4 * e + d])
            sh_ref[g, 128 * k : 128 * k + 64] = hi
            sl_ref[g, 128 * k : 128 * k + 64] = lo
            hi, lo = split2(sb_ref[4 * d + e])
            sh_ref[g, 128 * k + 64 : 128 * k + 128] = hi
            sl_ref[g, 128 * k + 64 : 128 * k + 128] = lo

    @pl.when(g == 0)
    def _():
        for k in range(2):
            hi, lo = split2(panel_ref[chunk_of(meta, 2 * q + k)])
            ph_ref[128 * k : 128 * k + 128] = hi
            pl_ref[128 * k : 128 * k + 128] = lo

    def assembled(k, j):
        tile_row = 8 * (4 * g + k) + row
        tile_col = 16 * (2 * q + j) + col
        at = tile_row - meta[16 * g]
        at_col = tile_col - meta[16 * q]
        use = (at >= 0) & (at < 16) & (at_col >= 0) & (at_col < 16) & (g >= q)
        index = jnp.where(use, g * (g + 1) + (at >> 3) * (g + 1) + q, 0)
        tile = parent_ref[k, 0, j, 0] + jnp.where(use, moved_ref[index], 0.0)
        return tile, (tile_row >= tile_col) & (tile_col >= start + PANEL_T)

    first_col = 32 * q + col
    active = (32 * g + 24 + row >= first_col) & (first_col + 16 >= start + PANEL_T)

    @pl.when(active)
    def _():
        trailing = dot3((sh_ref[g], sl_ref[g]), (ph_ref[...], pl_ref[...]), NT)
        for k in range(4):
            for j in range(2):
                tile, window = assembled(k, j)
                part = trailing[128 * k : 128 * k + 128, 128 * j : 128 * j + 128]
                out_ref[k, 0, j, 0] = tile - jnp.where(window, part, 0.0)

    @pl.when(jnp.logical_not(active))
    def _():
        for k in range(4):
            for j in range(2):
                out_ref[k, 0, j, 0] = assembled(k, j)[0]


def trailing_update(meta, parent_tiles, moved, sa, sb, panel):
    whole = pl.BlockSpec(memory_space=pltpu.VMEM)
    tiles = pl.BlockSpec((4, 1, 2, 1, 128, 128), lambda q, g, meta: (g, 0, q, 0, 0, 0))
    return pl.pallas_call(
        trailing_kernel,
        grid_spec=pltpu.PrefetchScalarGridSpec(
            num_scalar_prefetch=1,
            grid=(4, 4),
            in_specs=[tiles, whole, whole, whole, whole],
            out_specs=tiles,
            scratch_shapes=[
                pltpu.VMEM((4, 512, 512), BF16),
                pltpu.VMEM((4, 512, 512), BF16),
                pltpu.VMEM((256, 512), BF16),
                pltpu.VMEM((256, 512), BF16),
            ],
        ),
        out_shape=jax.ShapeDtypeStruct(parent_tiles.shape, F32),
        compiler_params=pltpu.CompilerParams(vmem_limit_bytes=40 << 20),
        cost_estimate=pl.CostEstimate(flops=7 * 10**9, bytes_accessed=24 << 20, transcendentals=0),
    )(meta, parent_tiles, moved, sa, sb, panel)


def per_device(
    contribution,
    parent_tiles,
    row_basis,
    pivot_basis,
    tile_ranks,
    block_map,
    panel_start,
    pivot_inverse,
):
    my_row = lax.axis_index("row")
    my_col = lax.axis_index("col")
    meta = jnp.concatenate(
        [block_map, tile_ranks, panel_start, jnp.stack([my_row, my_col])]
    ).astype(jnp.int32)
    shifts = [block_map[16 * u] - 32 * u for u in range(4)]

    pivots = gather_rows(pivot_basis[:, 0])
    by_row = [
        rotate(contribution[2 * u : 2 * u + 2, 0, 0 : u + 1, 0], "row", 8, shifts[u] & 7)
        for u in (3, 2, 1, 0)
    ][::-1]
    bases = gather_rows(row_basis[:, 0])
    parts = products(meta, pivots)
    wa = scatter_sums(parts[0:4], lambda v, d: col_perm(v, 0, d), lambda v, d: col_perm(v, d, 0))
    wb = scatter_sums(parts[4:8], lambda v, d: col_perm(v, d, 0), lambda v, d: col_perm(v, 0, d))
    cols = [
        rotate(
            jnp.concatenate([by_row[u][:, s] for u in range(s, 4)]), "col", 16, shifts[s]
        )
        for s in range(4)
    ]
    moved, panel_col = moved_tiles(meta, wa, wb, bases, cols, parent_tiles)
    got = lax.all_to_all(panel_col, "col", split_axis=0, concat_axis=0, tiled=True)
    panel, sa, sb = scale_panel(meta, got, pivot_inverse)

    turn = []
    for r in range(8):
        for c in range(16):
            turn.append((16 * r + c, 16 * (c // 2) + 8 * (c % 2) + r))
    panel = gather_rows(lax.ppermute(panel, ("row", "col"), turn))
    ring_a = jnp.stack([sa] + [col_perm(sa, 0, d) for d in (1, 2, 3)])
    ring_b = jnp.stack([sb] + [col_perm(sb, d, 0) for d in (1, 2, 3)])
    sa = jnp.concatenate([ring_a] + [col_perm(ring_a, d, 0) for d in (1, 2, 3)])
    sb = jnp.concatenate([ring_b] + [col_perm(ring_b, 0, d) for d in (1, 2, 3)])
    return trailing_update(meta, parent_tiles, moved, sa, sb, panel)


def solution(mesh):
    placed = (
        P(None, "row", None, "col", None, None),
        P(None, "row", None, "col", None, None),
        P(None, "row", None, None),
        P(None, "row", None, "col"),
        P(),
        P(),
        P(),
        P(),
    )
    return jax.shard_map(
        per_device,
        mesh=mesh,
        in_specs=placed,
        out_specs=P(None, "row", None, "col", None, None),
        check_vma=False,
    )
```

time: 820 us -> 342 us (0.42)
  waiting for transfers between devices: 634 us -> 162 us
  starting transfers between devices: 3.3 us -> 81.6 us
  matrix products: 66.6 us -> 0 us
  local copies, waits for them, and re-layouts: 62.5 us -> 23 us
  Pallas kernels: 0 us -> 30.2 us
  other arithmetic: 29.3 us -> 9.61 us
  blocking collectives: 0 us -> 18.1 us
  loops' own time: 0 us -> 10.8 us
  between operations: 14.7 us -> 4.58 us
    psum x3 -> x0, waiting for transfers between devices: 217 us -> none  [spread_2(): return lax.psum(jnp.where(mine, x, jnp.zeros_like(x)), axis)]
    ppermute x7 -> x45, waiting for transfers between devices: 306 us -> 162 us  [the longest x8 87.4 us: step(): return (lambda v: lax.ppermute(v, axis, pairs)) if k else lambda v: v]
    reduce_scatter x1 -> x0, waiting for transfers between devices: 81.2 us -> none  [per_device(): lax.psum_scatter(products.reshape(lax.axis_size('col') * local_cols, loca...]
    ppermute x7 -> x45, starting transfers between devices: 2.92 us -> 81.6 us  [the longest x24 36.6 us: col_perm(): return lax.ppermute(x, 'col', pairs)]
    dot_general x7 -> x0, matrix products: 66.6 us -> none  [the longest x1 18 us: per_device(): jnp.einsum('axq,byq->abxy', scaled, col_panel, precision=highest, preferr...]
    pallas_call x0 -> x4, Pallas kernels: none -> 30.2 us  [the longest x1 14.6 us: trailing_update(): pl.pallas_call(trailing_kernel, grid_spec=pltpu.PrefetchScalarGridSpec(nu...]
    all_gather x1 -> x0, waiting for transfers between devices: 29.4 us -> none  [per_device(): all_pivots = lax.all_gather(pivot_basis, 'row', axis=1, tiled=True)]
    all_to_all x0 -> x1, blocking collectives: none -> 18.1 us  [per_device(): lax.all_to_all(panel_col, 'col', split_axis=0, concat_axis=0, tiled=True)]
  transfers between devices with their start and end apart: 12 -> 45, of which waited for: 12 -> 21; matrix products, arithmetic and copies ran while one was open for 2% -> 8% of each run, Pallas kernels for 0% -> 4%
where the time goes in v1:
time: 342 us; the launch traced here: 340 us
  waiting for transfers between devices  162 us (47%)
  starting transfers between devices  81.6 us (24%)
  Pallas kernels  30.2 us (9%)
  local copies, waits for them, and re-layouts  23 us (7%)
  blocking collectives  18.1 us (5%)
  loops' own time  10.8 us (3%)
  other arithmetic  9.61 us (3%)
  between operations  4.58 us (1%)
    ppermute x8, waiting for transfers between devices, step(): return (lambda v: lax.ppermute(v, axis, pairs)) if k else lambda v: v  87.4 us
    ppermute x24, waiting for transfers between devices, col_perm(): return lax.ppermute(x, 'col', pairs)  52.2 us
    ppermute x24, starting transfers between devices, col_perm(): return lax.ppermute(x, 'col', pairs)  36.6 us
    ppermute x12, starting transfers between devices, row_perm(): return lax.ppermute(x, 'row', pairs)  35.6 us
    ppermute x12, waiting for transfers between devices, row_perm(): return lax.ppermute(x, 'row', pairs)  22.7 us
    all_to_all x1, blocking collectives, per_device(): lax.all_to_all(panel_col, 'col', split_axis=0, concat_axis=0, tiled=True)  18.1 us
    pallas_call x1, Pallas kernels, trailing_update(): pl.pallas_call(trailing_kernel, grid_spec=pltpu.PrefetchScalarGridSpec(nu...  14.6 us
    pallas_call x1, Pallas kernels, products(): pl.pallas_call(products_kernel, grid_spec=pltpu.PrefetchScalarGridSpec(nu...  12.7 us
  transfers between devices with their start and end apart: 45, of which 21 were waited for; matrix products, arithmetic and copies ran while one was open for 8% of the time, Pallas kernels for 4%

profile of v1, /device:TPU:0, one launch (start us, length us, event | category | flops | bytes accessed | tf_op | source)
XLA Modules:
  0.0 340.1 jit_solution(12111722114556958411)
XLA Ops:
  10.8 15.0 %collective-permute-done.90 = f32[8,64,128]{2,1,0:T(8,128)S(1)} collective-permute-done((f32[8,64,128]{2,1,0:T(8,128)}, f32[8,64,128]{2,1,0:T(8,128)S(1)}, u32[]{:S(2)}, u32[]{:S(2)}) %collective-permute-start.90) | collective-permute-done | bytes 262176 | tf_op jit(solution)/shard_map/ppermute | solution.py:52
  31.8 8.0 %conditional.8 = (f32[2,128,128]{2,1,0:T(8,128)}) conditional(s32[]{:T(128)} %bitcast.84, (f32[8,1,4,1,128,128]{5,4,3,2,1,0:T(8,128)S(1)}) %tuple.491, (f32[8,1,4,1,128,128]{5,4,3,2,1,0:T(8,128)S(1)}) %tuple.492, (f32[8,1,4,1,128,128]{5,4,3,2,1,0:T(8,128)S(1)}) %tuple.493, ...), branch_computations={%region_0.0_spmd, %region_1.0_spmd, %region_2.0_spmd, %region_3.0_... | conditional | bytes 786480 | solution.py:70
  39.7 9.6 %conditional.10 = (f32[2,3,128,128]{3,2,1,0:T(8,128)}) conditional(s32[]{:T(128)} %bitcast.88, (f32[8,1,4,1,128,128]{5,4,3,2,1,0:T(8,128)}) %tuple.351, (f32[8,1,4,1,128,128]{5,4,3,2,1,0:T(8,128)}) %tuple.351, (f32[8,1,4,1,128,128]{5,4,3,2,1,0:T(8,128)}) %tuple.351, (f32[8,1,4,1,128,128]{5,4,3,2,1,0:T(8,128)}) %tuple.351, ...), branch_computations={%region_16.0_spmd, %region_17.0_spmd, %region_18.0_spmd, %region_1... | conditional | bytes 2359344 | solution.py:70
  40.8 8.5 %collective-permute-done.60 = f32[2,3,128,128]{3,2,1,0:T(8,128)} collective-permute-done((f32[2,3,128,128]{3,2,1,0:T(8,128)S(1)}, f32[2,3,128,128]{3,2,1,0:T(8,128)}, u32[]{:S(2)}, u32[]{:S(2)}) %collective-permute-start.60) | collective-permute-done | bytes 393248 | tf_op jit(solution)/shard_map/cond/branch_1_fun/ppermute | solution.py:68
  49.3 15.9 %conditional.11 = (f32[2,4,128,128]{3,2,1,0:T(8,128)}) conditional(s32[]{:T(128)} %bitcast.90, (f32[8,1,4,1,128,128]{5,4,3,2,1,0:T(8,128)}) %tuple.351, (f32[8,1,4,1,128,128]{5,4,3,2,1,0:T(8,128)}) %tuple.351, (f32[8,1,4,1,128,128]{5,4,3,2,1,0:T(8,128)}) %tuple.351, (f32[8,1,4,1,128,128]{5,4,3,2,1,0:T(8,128)}) %tuple.351, ...), branch_computations={%region_24.0_spmd, %region_25.0_spmd, %region_26.0_spmd, %region_2... | conditional | bytes 3145776 | solution.py:70
  50.5 14.8 %collective-permute-done.69 = f32[2,4,128,128]{3,2,1,0:T(8,128)} collective-permute-done((f32[2,4,128,128]{3,2,1,0:T(8,128)S(1)}, f32[2,4,128,128]{3,2,1,0:T(8,128)}, u32[]{:S(2)}, u32[]{:S(2)}) %collective-permute-start.69) | collective-permute-done | bytes 524320 | tf_op jit(solution)/shard_map/cond/branch_3_fun/ppermute | solution.py:68
  65.2 19.2 %conditional.9 = (f32[2,2,128,128]{3,2,1,0:T(8,128)S(1)}, f32[2,1,128,128]{3,2,1,0:T(8,128)}, f32[2,1,128,128]{3,2,1,0:T(8,128)}, f32[2,128,128]{2,1,0:T(8,128)S(1)}, f32[2,128,128]{2,1,0:T(8,128)S(1)}) conditional(s32[]{:T(128)} %bitcast.85, f32[2,2,128,128]{3,2,1,0:T(8,128)S(1)} %slice_bitcast_fusion.24, ...), branch_computations={%region_8.0_spmd, %region_9.0_spmd, %region_10.0_spmd, %region_11.... | conditional | bytes 2621520 | solution.py:70
  88.4 12.7 %shard_map.82 = (f32[4,320,128]{2,1,0:T(8,128)S(1)}, f32[4,320,128]{2,1,0:T(8,128)}, f32[4,320,128]{2,1,0:T(8,128)}, f32[4,320,128]{2,1,0:T(8,128)}, f32[4,320,1...) custom-call(s32[131]{0:T(256)S(1)} %concatenate.176.meta, ...), custom_call_target="tpu_custom_call" | custom-call | flops 2000000000 | bytes 8388608 | tf_op jit(solution)/shard_map/pallas_call | solution.py:121
  114.0 20.6 %conditional.15 = (f32[2,128,128]{2,1,0:T(8,128)}) conditional(s32[]{:T(128)} %bitcast.98, f32[2,128,128]{2,1,0:T(8,128)} %get-tuple-element.313, f32[2,128,128]{2,1,0:T(8,128)} %get-tuple-element.313, f32[2,128,128]{2,1,0:T(8,128)} %get-tuple-element.313, f32[2,128,128]{2,1,0:T(8,128)} %get-tuple-element.313, ...), branch_computations={%region_80.0_spmd, %region_81.0_spmd, %region_82.0_spmd, %region_8... | conditional | bytes 786480 | solution.py:70
  114.2 19.8 %collective-permute-done.47 = f32[2,128,128]{2,1,0:T(8,128)S(1)} collective-permute-done((f32[2,128,128]{2,1,0:T(8,128)}, f32[2,128,128]{2,1,0:T(8,128)S(1)}, u32[]{:S(2)}, u32[]{:S(2)}) %collective-permute-start.47) | collective-permute-done | bytes 131104 | tf_op jit(solution)/shard_map/cond/branch_3_fun/ppermute | solution.py:68
  134.6 12.3 %conditional.14 = (f32[4,128,128]{2,1,0:T(8,128)}) conditional(s32[]{:T(128)} %bitcast.95, f32[4,128,128]{2,1,0:T(8,128)} %pad_maximum_fusion.7, f32[4,128,128]{2,1,0:T(8,128)} %pad_maximum_fusion.7, f32[4,128,128]{2,1,0:T(8,128)} %pad_maximum_fusion.7, f32[4,128,128]{2,1,0:T(8,128)} %pad_maximum_fusion.7, ...), branch_computations={%region_64.0_spmd, %region_65.0_spmd, %region_66.0_spmd, %region_6... | conditional | bytes 1572912 | solution.py:70
  134.7 11.2 %collective-permute-done.38 = f32[4,128,128]{2,1,0:T(8,128)S(1)} collective-permute-done((f32[4,128,128]{2,1,0:T(8,128)}, f32[4,128,128]{2,1,0:T(8,128)S(1)}, u32[]{:S(2)}, u32[]{:S(2)}) %collective-permute-start.38) | collective-permute-done | bytes 262176 | tf_op jit(solution)/shard_map/cond/branch_9_fun/ppermute | solution.py:68
  146.9 16.8 %conditional.12 = (f32[8,128,128]{2,1,0:T(8,128)}) conditional(s32[]{:T(128)} %bitcast.83, f32[8,128,128]{2,1,0:T(8,128)} %pad_maximum_fusion.3, f32[8,128,128]{2,1,0:T(8,128)} %pad_maximum_fusion.3, f32[8,128,128]{2,1,0:T(8,128)} %pad_maximum_fusion.3, f32[8,128,128]{2,1,0:T(8,128)} %pad_maximum_fusion.3, ...), branch_computations={%region_32.0_spmd, %region_33.0_spmd, %region_34.0_spmd, %region_3... | conditional | bytes 3145776 | solution.py:70
  149.4 13.6 %collective-permute-done.9 = f32[8,128,128]{2,1,0:T(8,128)S(1)} collective-permute-done((f32[8,128,128]{2,1,0:T(8,128)}, f32[8,128,128]{2,1,0:T(8,128)S(1)}, u32[]{:S(2)}, u32[]{:S(2)}) %collective-permute-start.9) | collective-permute-done | bytes 524320 | tf_op jit(solution)/shard_map/cond/branch_10_fun/ppermute | solution.py:68
  163.8 12.1 %conditional.13 = (f32[6,128,128]{2,1,0:T(8,128)}) conditional(s32[]{:T(128)} %bitcast.92, f32[6,128,128]{2,1,0:T(8,128)} %pad_maximum_fusion.6, f32[6,128,128]{2,1,0:T(8,128)} %pad_maximum_fusion.6, f32[6,128,128]{2,1,0:T(8,128)} %pad_maximum_fusion.6, f32[6,128,128]{2,1,0:T(8,128)} %pad_maximum_fusion.6, ...), branch_computations={%region_48.0_spmd, %region_49.0_spmd, %region_50.0_spmd, %region_5... | conditional | bytes 2359344 | solution.py:70
  167.9 7.2 %collective-permute-done.28 = f32[6,128,128]{2,1,0:T(8,128)S(1)} collective-permute-done((f32[6,128,128]{2,1,0:T(8,128)}, f32[6,128,128]{2,1,0:T(8,128)S(1)}, u32[]{:S(2)}, u32[]{:S(2)}) %collective-permute-start.28) | collective-permute-done | bytes 393248 | tf_op jit(solution)/shard_map/cond/branch_14_fun/ppermute | solution.py:68
  185.8 8.9 %collective-permute-done.98 = f32[4,320,128]{2,1,0:T(8,128)S(1)} collective-permute-done((f32[4,320,128]{2,1,0:T(8,128)}, f32[4,320,128]{2,1,0:T(8,128)S(1)}, u32[]{:S(2)}, u32[]{:S(2)}) %collective-permute-start.98) | collective-permute-done | bytes 655392 | tf_op jit(solution)/shard_map/ppermute | solution.py:57
  196.7 14.3 %collective-permute-done.99 = f32[4,320,128]{2,1,0:T(8,128)S(1)} collective-permute-done((f32[4,320,128]{2,1,0:T(8,128)}, f32[4,320,128]{2,1,0:T(8,128)S(1)}, u32[]{:S(2)}, u32[]{:S(2)}) %collective-permute-start.99) | collective-permute-done | bytes 655392 | tf_op jit(solution)/shard_map/ppermute | solution.py:57
  230.1 18.1 %all_to_all.5.got_ref = f32[16,128,128]{2,1,0:T(8,128)S(1)} all-to-all(f32[16,128,128]{2,1,0:T(8,128)S(1)} %get-tuple-element.234), channel_id=1, replica_groups=mesh['row'=8,'col'=16] {'col'}, dimensions={0} | all-to-all | bytes 2097152 | tf_op jit(solution)/shard_map/all_to_all | solution.py:385
  264.9 26.5 %collective-permute-start.123 = (f32[128,512]{1,0:T(8,128)S(1)}, f32[128,512]{1,0:T(8,128)S(1)}, u32[]{:S(2)}, u32[]{:S(2)}) collective-permute-start(f32[128,512]{1,0:T(8,128)S(1)} %collective-permute-done.120), channel_id=1, source_target_pairs={{0,96},{16,112},{32,0},{48,16},{64,32},{80,48},{96,64},{112,80},{1... | collective-permute-start | bytes 786440 | tf_op jit(solution)/shard_map/ppermute | solution.py:52
  292.4 7.3 %collective-permute-done.123 = f32[128,512]{1,0:T(8,128)S(1)} collective-permute-done((f32[128,512]{1,0:T(8,128)S(1)}, f32[128,512]{1,0:T(8,128)S(1)}, u32[]{:S(2)}, u32[]{:S(2)}) %collective-permute-start.123) | collective-permute-done | bytes 262176 | tf_op jit(solution)/shard_map/ppermute | solution.py:52
  303.8 9.7 %collective-permute-done.111 = f32[4,64,512]{2,1,0:T(8,128)S(1)} collective-permute-done((f32[4,64,512]{2,1,0:T(8,128)S(1)}, f32[4,64,512]{2,1,0:T(8,128)S(1)}, u32[]{:S(2)}, u32[]{:S(2)}) %collective-permute-start.111) | collective-permute-done | bytes 524320 | tf_op jit(solution)/shard_map/ppermute | solution.py:57
  313.7 11.4 %collective-permute-done.117 = f32[4,64,512]{2,1,0:T(8,128)S(1)} collective-permute-done((f32[4,64,512]{2,1,0:T(8,128)S(1)}, f32[4,64,512]{2,1,0:T(8,128)S(1)}, u32[]{:S(2)}, u32[]{:S(2)}) %collective-permute-start.117) | collective-permute-done | bytes 524320 | tf_op jit(solution)/shard_map/ppermute | solution.py:57
  325.4 14.6 %shard_map.85 = f32[16,1,8,1,128,128]{5,4,3,2,1,0:T(8,128)} custom-call(s32[131]{0:T(256)S(1)} %concatenate.176.meta, f32[16,1,8,1,128,128]{5,4,3,2,1,0:T(8,128)} %parent_ref.1, f32[20,128,128]{2,1,0:T(8,128)S(1)} %get-tuple-element.233.moved_ref, f32[16,64,512]{2,1,0:T(8,128)S(1)} %constant_dynamic-update-slice_fusion.10.sa_ref, ...), custom_call_target="tpu_custom_call" | custom-call | flops 7000000000 | bytes 25165824 | tf_op jit(solution)/shard_map/pallas_call | solution.py:332
  (173 shorter events, 111.1 us)
Async XLA Ops:
  0.0 109.2 %collective-permute-start.106 = (f32[8,64,128]{2,1,0:T(8,128)}, f32[8,64,128]{2,1,0:T(8,128)}, u32[]{:S(2)}, u32[]{:S(2)}) collective-permute-start(f32[8,64,128]{2,1,0:T(8,128)} %bitcast.209), channel_id=1, source_target_pairs={{0,96},{16,112},{32,0},{48,16},{64,32},{80,48},{96,64},{112,80},{1... | collective-permute-start | bytes 786440 | tf_op jit(solution)/shard_map/ppermute | solution.py:52
  3.1 107.2 %collective-permute-start.105 = (f32[8,64,128]{2,1,0:T(8,128)}, f32[8,64,128]{2,1,0:T(8,128)}, u32[]{:S(2)}, u32[]{:S(2)}) collective-permute-start(f32[8,64,128]{2,1,0:T(8,128)} %bitcast.210), channel_id=1, source_target_pairs={{0,64},{16,80},{32,96},{48,112},{64,0},{80,16},{96,32},{112,48},{1... | collective-permute-start | bytes 786440 | tf_op jit(solution)/shard_map/ppermute | solution.py:52
  3.7 22.1 %collective-permute-start.90 = (f32[8,64,128]{2,1,0:T(8,128)}, f32[8,64,128]{2,1,0:T(8,128)S(1)}, u32[]{:S(2)}, u32[]{:S(2)}) collective-permute-start(f32[8,64,128]{2,1,0:T(8,128)} %bitcast.205), channel_id=1, source_target_pairs={{0,96},{16,112},{32,0},{48,16},{64,32},{80,48},{96,64},{112,80},{1... | collective-permute-start | bytes 786440 | tf_op jit(solution)/shard_map/ppermute | solution.py:52
  4.7 21.1 %collective-permute-start.89 = (f32[8,64,128]{2,1,0:T(8,128)}, f32[8,64,128]{2,1,0:T(8,128)S(1)}, u32[]{:S(2)}, u32[]{:S(2)}) collective-permute-start(f32[8,64,128]{2,1,0:T(8,128)} %bitcast.206), channel_id=1, source_target_pairs={{0,64},{16,80},{32,96},{48,112},{64,0},{80,16},{96,32},{112,48},{1... | collective-permute-start | bytes 786440 | tf_op jit(solution)/shard_map/ppermute | solution.py:52
  6.8 19.1 %collective-permute-start.88 = (f32[8,64,128]{2,1,0:T(8,128)}, f32[8,64,128]{2,1,0:T(8,128)S(1)}, u32[]{:S(2)}, u32[]{:S(2)}) collective-permute-start(f32[8,64,128]{2,1,0:T(8,128)} %bitcast.207), channel_id=1, source_target_pairs={{0,32},{16,48},{32,64},{48,80},{64,96},{80,112},{96,0},{112,16},{1... | collective-permute-start | bytes 786440 | tf_op jit(solution)/shard_map/ppermute | solution.py:52
  25.8 84.5 %collective-permute-start.104 = (f32[8,64,128]{2,1,0:T(8,128)}, f32[8,64,128]{2,1,0:T(8,128)}, u32[]{:S(2)}, u32[]{:S(2)}) collective-permute-start(f32[8,64,128]{2,1,0:T(8,128)} %bitcast.211), channel_id=1, source_target_pairs={{0,32},{16,48},{32,64},{48,80},{64,96},{80,112},{96,0},{112,16},{1... | collective-permute-start | bytes 786440 | tf_op jit(solution)/shard_map/ppermute | solution.py:52
  28.7 59.5 %collective-permute-start.91 = (f32[4,8,64,128]{3,2,1,0:T(8,128)}, f32[4,8,64,128]{3,2,1,0:T(8,128)S(1)}, u32[]{:S(2)}, u32[]{:S(2)}) collective-permute-start(f32[4,8,64,128]{3,2,1,0:T(8,128)} %pad_maximum_fusion), channel_id=1, source_target_pairs={{0,16},{16,0},{32,48},{48,32},{64,80},{80,64},{96,112},{112,96},{1... | collective-permute-start | bytes 3145736 | tf_op jit(solution)/shard_map/ppermute | solution.py:52
  101.2 76.2 %collective-permute-start.92 = (f32[4,320,128]{2,1,0:T(8,128)}, f32[4,320,128]{2,1,0:T(8,128)}, u32[]{:S(2)}, u32[]{:S(2)}) collective-permute-start(f32[4,320,128]{2,1,0:T(8,128)} %get-tuple-element.224), channel_id=1, source_target_pairs={{0,1},{1,2},{2,3},{3,0},{4,5},{5,6},{6,7},{7,4},{8,9},{9,10},{10,1... | collective-permute-start | bytes 1966088 | tf_op jit(solution)/shard_map/ppermute | solution.py:57
  103.1 78.3 %collective-permute-start.93 = (f32[4,320,128]{2,1,0:T(8,128)}, f32[4,320,128]{2,1,0:T(8,128)}, u32[]{:S(2)}, u32[]{:S(2)}) collective-permute-start(f32[4,320,128]{2,1,0:T(8,128)} %get-tuple-element.225), channel_id=1, source_target_pairs={{0,2},{1,3},{2,0},{3,1},{4,6},{5,7},{6,4},{7,5},{8,10},{9,11},{10,... | collective-permute-start | bytes 1966088 | tf_op jit(solution)/shard_map/ppermute | solution.py:57
  109.2 74.1 %collective-permute-start.94 = (f32[4,320,128]{2,1,0:T(8,128)}, f32[4,320,128]{2,1,0:T(8,128)}, u32[]{:S(2)}, u32[]{:S(2)}) collective-permute-start(f32[4,320,128]{2,1,0:T(8,128)} %get-tuple-element.226), channel_id=1, source_target_pairs={{0,3},{1,0},{2,1},{3,2},{4,7},{5,4},{6,5},{7,6},{8,11},{9,8},{10,9... | collective-permute-start | bytes 1966088 | tf_op jit(solution)/shard_map/ppermute | solution.py:57
  112.6 103.8 %collective-permute-start.107 = (f32[4,8,64,128]{3,2,1,0:T(8,128)}, f32[4,8,64,128]{3,2,1,0:T(8,128)}, u32[]{:S(2)}, u32[]{:S(2)}) collective-permute-start(f32[4,8,64,128]{3,2,1,0:T(8,128)} %pad_maximum_fusion.1), channel_id=1, source_target_pairs={{0,16},{16,0},{32,48},{48,32},{64,80},{80,64},{96,112},{112,96},{1... | collective-permute-start | bytes 3145736 | tf_op jit(solution)/shard_map/ppermute | solution.py:52
  114.1 19.9 %collective-permute-start.47 = (f32[2,128,128]{2,1,0:T(8,128)}, f32[2,128,128]{2,1,0:T(8,128)S(1)}, u32[]{:S(2)}, u32[]{:S(2)}) collective-permute-start(f32[2,128,128]{2,1,0:T(8,128)} %param.83), channel_id=1, source_target_pairs={{0,3},{1,4},{2,5},{3,6},{4,7},{5,8},{6,9},{7,10},{8,11},{9,12},{10... | collective-permute-start | bytes 393224 | tf_op jit(solution)/shard_map/cond/branch_3_fun/ppermute | solution.py:68
  147.0 16.0 %collective-permute-start.9 = (f32[8,128,128]{2,1,0:T(8,128)}, f32[8,128,128]{2,1,0:T(8,128)S(1)}, u32[]{:S(2)}, u32[]{:S(2)}) collective-permute-start(f32[8,128,128]{2,1,0:T(8,128)} %param.42), channel_id=1, source_target_pairs={{0,10},{1,11},{2,12},{3,13},{4,14},{5,15},{6,0},{7,1},{8,2},{9,3},... | collective-permute-start | bytes 1572872 | tf_op jit(solution)/shard_map/cond/branch_10_fun/ppermute | solution.py:68
  175.9 18.8 %collective-permute-start.98 = (f32[4,320,128]{2,1,0:T(8,128)}, f32[4,320,128]{2,1,0:T(8,128)S(1)}, u32[]{:S(2)}, u32[]{:S(2)}) collective-permute-start(f32[4,320,128]{2,1,0:T(8,128)} %copy-done.4), channel_id=1, source_target_pairs={{0,4},{1,5},{2,6},{3,7},{4,8},{5,9},{6,10},{7,11},{8,12},{9,13},{1... | collective-permute-start | bytes 1966088 | tf_op jit(solution)/shard_map/ppermute | solution.py:57
  177.4 33.7 %collective-permute-start.99 = (f32[4,320,128]{2,1,0:T(8,128)}, f32[4,320,128]{2,1,0:T(8,128)S(1)}, u32[]{:S(2)}, u32[]{:S(2)}) collective-permute-start(f32[4,320,128]{2,1,0:T(8,128)} %copy-done.3), channel_id=1, source_target_pairs={{0,8},{1,9},{2,10},{3,11},{4,12},{5,13},{6,14},{7,15},{8,0},{9,1},... | collective-permute-start | bytes 1966088 | tf_op jit(solution)/shard_map/ppermute | solution.py:57
  181.4 29.7 %collective-permute-start.100 = (f32[4,320,128]{2,1,0:T(8,128)}, f32[4,320,128]{2,1,0:T(8,128)S(1)}, u32[]{:S(2)}, u32[]{:S(2)}) collective-permute-start(f32[4,320,128]{2,1,0:T(8,128)} %copy-done.2), channel_id=1, source_target_pairs={{0,12},{1,13},{2,14},{3,15},{4,0},{5,1},{6,2},{7,3},{8,4},{9,5},{1... | collective-permute-start | bytes 1966088 | tf_op jit(solution)/shard_map/ppermute | solution.py:57
  185.1 31.2 %collective-permute-start.97 = (f32[320,128]{1,0:T(8,128)S(1)}, f32[320,128]{1,0:T(8,128)S(1)}, u32[]{:S(2)}, u32[]{:S(2)}) collective-permute-start(f32[320,128]{1,0:T(8,128)S(1)} %get-tuple-element.309), channel_id=1, source_target_pairs={{0,12},{1,13},{2,14},{3,15},{4,0},{5,1},{6,2},{7,3},{8,4},{9,5},{1... | collective-permute-start | bytes 491528 | tf_op jit(solution)/shard_map/ppermute | solution.py:57
  194.7 24.9 %collective-permute-start.96 = (f32[320,128]{1,0:T(8,128)S(1)}, f32[320,128]{1,0:T(8,128)S(1)}, u32[]{:S(2)}, u32[]{:S(2)}) collective-permute-start(f32[320,128]{1,0:T(8,128)S(1)} %get-tuple-element.310), channel_id=1, source_target_pairs={{0,8},{1,9},{2,10},{3,11},{4,12},{5,13},{6,14},{7,15},{8,0},{9,1},... | collective-permute-start | bytes 491528 | tf_op jit(solution)/shard_map/ppermute | solution.py:57
  258.2 55.4 %collective-permute-start.113 = (f32[4,64,512]{2,1,0:T(8,128)S(1)}, f32[4,64,512]{2,1,0:T(8,128)S(1)}, u32[]{:S(2)}, u32[]{:S(2)}) collective-permute-start(f32[4,64,512]{2,1,0:T(8,128)S(1)} %pad_maximum_fusion.4), channel_id=1, source_target_pairs={{0,12},{1,13},{2,14},{3,15},{4,0},{5,1},{6,2},{7,3},{8,4},{9,5},{1... | collective-permute-start | bytes 1572872 | tf_op jit(solution)/shard_map/ppermute | solution.py:57
  264.8 38.7 %collective-permute-start.112 = (f32[4,64,512]{2,1,0:T(8,128)S(1)}, f32[4,64,512]{2,1,0:T(8,128)S(1)}, u32[]{:S(2)}, u32[]{:S(2)}) collective-permute-start(f32[4,64,512]{2,1,0:T(8,128)S(1)} %pad_maximum_fusion.4), channel_id=1, source_target_pairs={{0,8},{1,9},{2,10},{3,11},{4,12},{5,13},{6,14},{7,15},{8,0},{9,1},... | collective-permute-start | bytes 1572872 | tf_op jit(solution)/shard_map/ppermute | solution.py:57
  264.9 34.8 %collective-permute-start.123 = (f32[128,512]{1,0:T(8,128)S(1)}, f32[128,512]{1,0:T(8,128)S(1)}, u32[]{:S(2)}, u32[]{:S(2)}) collective-permute-start(f32[128,512]{1,0:T(8,128)S(1)} %collective-permute-done.120), channel_id=1, source_target_pairs={{0,96},{16,112},{32,0},{48,16},{64,32},{80,48},{96,64},{112,80},{1... | collective-permute-start | bytes 786440 | tf_op jit(solution)/shard_map/ppermute | solution.py:52
  300.0 25.1 %collective-permute-start.118 = (f32[4,64,512]{2,1,0:T(8,128)S(1)}, f32[4,64,512]{2,1,0:T(8,128)S(1)}, u32[]{:S(2)}, u32[]{:S(2)}) collective-permute-start(f32[4,64,512]{2,1,0:T(8,128)S(1)} %pad_maximum_fusion.5), channel_id=1, source_target_pairs={{0,2},{1,3},{2,0},{3,1},{4,6},{5,7},{6,4},{7,5},{8,10},{9,11},{10,... | collective-permute-start | bytes 1572872 | tf_op jit(solution)/shard_map/ppermute | solution.py:57
  303.3 22.0 %collective-permute-start.124 = (f32[4,128,512]{2,1,0:T(8,128)S(1)}, f32[4,128,512]{2,1,0:T(8,128)S(1)}, u32[]{:S(2)}, u32[]{:S(2)}) collective-permute-start(f32[4,128,512]{2,1,0:T(8,128)S(1)} %pad_maximum_fusion.2), channel_id=1, source_target_pairs={{0,16},{16,0},{32,48},{48,32},{64,80},{80,64},{96,112},{112,96},{1... | collective-permute-start | bytes 3145736 | tf_op jit(solution)/shard_map/ppermute | solution.py:52
  303.4 21.7 %collective-permute-start.117 = (f32[4,64,512]{2,1,0:T(8,128)S(1)}, f32[4,64,512]{2,1,0:T(8,128)S(1)}, u32[]{:S(2)}, u32[]{:S(2)}) collective-permute-start(f32[4,64,512]{2,1,0:T(8,128)S(1)} %pad_maximum_fusion.5), channel_id=1, source_target_pairs={{0,1},{1,2},{2,3},{3,0},{4,5},{5,6},{6,7},{7,4},{8,9},{9,10},{10,1... | collective-permute-start | bytes 1572872 | tf_op jit(solution)/shard_map/ppermute | solution.py:57
  (41 other events, 431.2 us)

commit v2 on v1

v2 whole, which is shorter than its diff:
```python
import jax
import jax.numpy as jnp
from jax import lax
from jax.experimental import pallas as pl
from jax.experimental.pallas import tpu as pltpu
from jax.sharding import PartitionSpec as P

PANEL_T = 4
F32 = jnp.float32
BF16 = jnp.bfloat16


def shift_of(meta, u):
    return meta[16 * u] - 32 * u


def gathered_row(meta, k):
    row = meta[129]
    return 2 * (((row >> 1) - k % 4) & 3) + ((row + k // 4) & 1)


def row_source(meta, u):
    return (meta[129] - shift_of(meta, u)) & 7


def col_source(meta, s, col):
    return (col - shift_of(meta, s)) & 15


def panel_child(meta, p):
    tile = meta[128] + p
    s = tile >> 5
    at = tile - meta[16 * s]
    return s, at & 15, (at >= 0) & (at < 16)


def split2(x):
    hi = x.astype(BF16)
    return hi, (x - hi.astype(F32)).astype(BF16)


def dot3(a, b, dims):
    dn = (dims, ((), ()))
    ah, al = a
    bh, bl = b
    low = lax.dot_general(ah, bl, dn, preferred_element_type=F32)
    low += lax.dot_general(al, bh, dn, preferred_element_type=F32)
    return lax.dot_general(ah, bh, dn, preferred_element_type=F32) + low


NT = ((1,), (1,))
NN = ((1,), (0,))
TN = ((0,), (0,))


def after(x, *others):
    return lax.optimization_barrier((x,) + others)[0]


def row_perm(x, dy, dc):
    pairs = [(2 * y + k, 2 * ((y + dy) % 4) + (k + dc) % 2) for y in range(4) for k in range(2)]
    return lax.ppermute(x, "row", pairs)


def col_perm(x, dx, dz):
    pairs = [(4 * a + b, 4 * ((a + dx) % 4) + (b + dz) % 4) for a in range(4) for b in range(4)]
    return lax.ppermute(x, "col", pairs)


def gather_rows(x):
    ring = [x] + [row_perm(x, d, 0) for d in (1, 2, 3)]
    return ring + [row_perm(v, 0, 1) for v in ring]


def rotate(x, axis, count, by):
    def step(k):
        pairs = [(i, (i + k) % count) for i in range(count)]
        return (lambda v: lax.ppermute(v, axis, pairs)) if k else (lambda v: v)

    return lax.switch(by, [step(k) for k in range(count)], x)


def across_col(x):
    return lax.all_to_all(x, "col", split_axis=0, concat_axis=0, tiled=True)


def whole():
    return pl.BlockSpec(memory_space=pltpu.VMEM)


def products_kernel(meta, *refs):
    v_refs, a_refs, b_refs = refs[0:8], refs[8:12], refs[12:16]
    vh_ref, vl_ref, hi_ref, lo_ref = refs[16:20]
    e = pl.program_id(0)

    @pl.when(e == 0)
    def _():
        for k in range(8):
            rho = gathered_row(meta, k)
            hi, lo = split2(v_refs[k][...])
            vh_ref[rho] = hi
            vl_ref[rho] = lo
        for u in range(4):
            rho = row_source(meta, u)
            for w in range(2):
                at = 128 * u + 64 * w
                hi_ref[at : at + 64] = vh_ref[rho, 2 * u + w]
                lo_ref[at : at + 64] = vl_ref[rho, 2 * u + w]

    def left(first, last):
        return hi_ref[first:last], lo_ref[first:last]

    def right(col, s, q):
        places = []
        for k in (s, q):
            j = col_source(meta, k, col)
            places.append((j & 7, 2 * k + (j >> 3)))
        return tuple(
            jnp.concatenate([ref[places[0]], ref[places[1]]], axis=0) for ref in (vh_ref, vl_ref)
        )

    col = meta[130]
    x, z = col >> 2, col & 3
    low_half = lax.broadcasted_iota(jnp.int32, (128, 128), 1) < 64
    for d in range(4):
        other = 4 * ((x + e) & 3) + ((z + d) & 3)
        a_refs[d][0] = dot3(left(128, 448), right(other, 0, 1), NT)
        other = 4 * ((x + d) & 3) + ((z + e) & 3)
        b_refs[d][0, 0:64] = dot3(left(448, 512), right(other, 0, 1), NT)
        ends = right(other, 0, 3)
        b_refs[d][0, 64:192] = jnp.where(
            low_half, dot3(left(0, 128), ends, NT), dot3(left(384, 512), ends, NT)
        )
        mid = right(other, 2, 2)
        b_refs[d][0, 192:320] = jnp.where(
            low_half, dot3(left(256, 384), mid, NT), dot3(left(384, 512), mid, NT)
        )


def products(meta, pivots):
    return pl.pallas_call(
        products_kernel,
        grid_spec=pltpu.PrefetchScalarGridSpec(
            num_scalar_prefetch=1,
            grid=(4,),
            in_specs=[whole()] * 8,
            out_specs=[pl.BlockSpec((1, 320, 128), lambda e, meta: (e, 0, 0))] * 8,
            scratch_shapes=[pltpu.VMEM((8, 8, 64, 128), BF16)] * 2
            + [pltpu.VMEM((512, 128), BF16)] * 2,
        ),
        out_shape=[jax.ShapeDtypeStruct((4, 320, 128), F32)] * 8,
        compiler_params=pltpu.CompilerParams(vmem_limit_bytes=24 << 20),
        cost_estimate=pl.CostEstimate(flops=2 * 10**9, bytes_accessed=8 << 20, transcendentals=0),
    )(meta, *pivots)


def scatter_sums(parts, first, second):
    arrived = [parts[0]] + [first(parts[d], d) for d in (1, 2, 3)]
    sums = [arrived[0][e] + arrived[1][e] + arrived[2][e] + arrived[3][e] for e in range(4)]
    return [sums[0]] + [second(sums[e], e) for e in (1, 2, 3)]


def send_kernel(meta, *refs):
    v_refs, c_refs, out_ref, v_ref = refs[0:8], refs[8:12], refs[12], refs[13]
    for k in range(8):
        v_ref[gathered_row(meta, k)] = v_refs[k][...]
    own = jnp.concatenate(
        [v_ref[row_source(meta, u), 2 * u + w] for u in range(4) for w in range(2)], axis=0
    )
    own = split2(own)

    def pair(p):
        parts = []
        for k in (p, p + 1):
            s, at, _ = panel_child(meta, k)
            parts.append(v_ref[at & 7, 2 * s + (at >> 3)])
        return split2(jnp.concatenate(parts, axis=0))

    first, second = dot3(own, pair(0), NT), dot3(own, pair(2), NT)
    start, col = meta[128], meta[130]
    mine = jnp.int32(0)
    for s in range(1, 4):
        p = meta[16 * s] + col - start
        mine = jnp.where((p >= 0) & (p < PANEL_T), s, mine)
    for u in range(4):
        rho = row_source(meta, u)
        for w in range(2):
            t = 2 * u + w
            slot = (meta[16 * u] + 8 * w + rho) >> 3
            out_ref[slot, 1, 0:64] = first[64 * t : 64 * t + 64]
            out_ref[slot, 1, 64:128] = second[64 * t : 64 * t + 64]
            out_ref[slot, 0] = c_refs[u][w, jnp.minimum(mine, u)]


def panel_send(meta, pivots, by_row):
    return pl.pallas_call(
        send_kernel,
        grid_spec=pltpu.PrefetchScalarGridSpec(
            num_scalar_prefetch=1,
            grid=(),
            in_specs=[whole()] * 12,
            out_specs=whole(),
            scratch_shapes=[pltpu.VMEM((8, 8, 64, 128), F32)],
        ),
        out_shape=jax.ShapeDtypeStruct((16, 2, 128, 128), F32),
        compiler_params=pltpu.CompilerParams(vmem_limit_bytes=24 << 20),
        cost_estimate=pl.CostEstimate(flops=5 * 10**8, bytes_accessed=5 << 20, transcendentals=0),
    )(meta, *pivots, *by_row)


def masked_basis(meta, ref, rho, t, tile):
    rows = lax.broadcasted_iota(jnp.int32, (64, 128), 0)
    return jnp.where(rows < meta[64 + tile], ref[rho, t], 0.0)


def block_diagonal(first, second):
    zero = jnp.zeros((64, 128), F32)
    top = jnp.concatenate([first, zero], axis=1)
    bottom = jnp.concatenate([zero, second], axis=1)
    return split2(jnp.concatenate([top, bottom], axis=0))


def panel_kernel(meta, *refs):
    base_refs, parent_ref, got_ref, inverse_ref = refs[0:8], refs[8], refs[9], refs[10]
    panel_ref, sa_ref, sb_ref, base_ref = refs[11:15]
    for k in range(8):
        base_ref[gathered_row(meta, k)] = base_refs[k][...]
    row, col, start = meta[129], meta[130], meta[128]
    u = col >> 2
    at = 8 * col + row - meta[16 * u]
    row_ok = (at >= 0) & (at < 16)
    at = at & 15
    tile = 16 * u + at
    bi = split2(masked_basis(meta, base_ref, at & 7, 2 * u + (at >> 3), tile))
    weights = got_ref[0, 1]
    for k in range(1, 16):
        weights = weights + got_ref[k, 1]
    bj, keep, place = [], [], []
    for p in range(PANEL_T):
        s, at_col, col_ok = panel_child(meta, p)
        other = 16 * s + at_col
        bj.append(masked_basis(meta, base_ref, at_col & 7, 2 * s + (at_col >> 3), other))
        keep.append(row_ok & col_ok & (tile >= other))
        place.append(at_col)
    half = [
        dot3(split2(weights[0:64]), block_diagonal(bj[0], bj[1]), NN),
        dot3(split2(weights[64:128]), block_diagonal(bj[2], bj[3]), NN),
    ]
    update = dot3(bi, split2(jnp.concatenate(half, axis=1)), TN)
    tiles = []
    for p in range(PANEL_T):
        moved = got_ref[place[p], 0] - update[:, 128 * p : 128 * p + 128]
        tiles.append(parent_ref[(start + p) & 15] + jnp.where(keep[p], moved, 0.0))
    panel = jnp.concatenate(tiles, axis=1)
    panel_ref[...] = panel
    out = dot3(split2(panel), split2(inverse_ref[...]), NN)
    sa_ref[...] = out[0:64]
    sb_ref[...] = out[64:128]


def panel_row(meta, bases, parent_panel, got, inverse):
    return pl.pallas_call(
        panel_kernel,
        grid_spec=pltpu.PrefetchScalarGridSpec(
            num_scalar_prefetch=1,
            grid=(),
            in_specs=[whole()] * 11,
            out_specs=[whole()] * 3,
            scratch_shapes=[pltpu.VMEM((8, 8, 64, 128), F32)],
        ),
        out_shape=[
            jax.ShapeDtypeStruct((128, 512), F32),
            jax.ShapeDtypeStruct((64, 512), F32),
            jax.ShapeDtypeStruct((64, 512), F32),
        ],
        compiler_params=pltpu.CompilerParams(vmem_limit_bytes=32 << 20),
        cost_estimate=pl.CostEstimate(flops=4 * 10**8, bytes_accessed=6 << 20, transcendentals=0),
    )(meta, *bases, parent_panel, got, inverse)


def moved_kernel(meta, *refs):
    wa, wb, base_refs, c_refs = refs[0:4], refs[4:8], refs[8:16], refs[16:20]
    out_ref, g_ref, base_ref = refs[20:23]
    for k in range(8):
        base_ref[gathered_row(meta, k)] = base_refs[k][...]
    col = meta[130]
    bj = []
    for s in range(4):
        j = col_source(meta, s, col)
        bj.append(masked_basis(meta, base_ref, j & 7, 2 * s + (j >> 3), 16 * s + j))
    d01, d03, d22 = (block_diagonal(bj[s], bj[q]) for s, q in ((0, 1), (0, 3), (2, 2)))
    a_sum = wa[0][...] + wa[1][...] + wa[2][...] + wa[3][...]
    b_sum = wb[0][...] + wb[1][...] + wb[2][...] + wb[3][...]
    g_ref[0:320] = dot3(split2(a_sum), d01, NN)
    g_ref[320:384] = dot3(split2(b_sum[0:64]), d01, NN)
    g_ref[384:512] = dot3(split2(b_sum[64:192]), d03, NN)
    g_ref[512:640] = dot3(split2(b_sum[192:320]), d22, NN)

    for t in range(8):
        u, w = t // 2, t % 2
        rho = row_source(meta, u)
        bi = split2(masked_basis(meta, base_ref, rho, t, 16 * u + 8 * w + rho))

        def put(s, tile):
            value = c_refs[s][2 * (u - s) + w] - tile
            if u == s:
                keep = rho + 8 * w >= col_source(meta, s, col)
                value = jnp.where(keep, value, 0.0)
            out_ref[u * (u + 1) + w * (u + 1) + s] = value

        def update(first, lane, wide):
            return dot3(bi, split2(g_ref[first : first + 64, lane : lane + wide]), TN)

        if t >= 2:
            both = update(64 * (t - 2), 0, 256)
            put(0, both[:, 0:128])
            put(1, both[:, 128:256])
        else:
            put(0, update(384 + 64 * t, 0, 128))
        if u == 2:
            put(2, update(512 + 64 * w, 0, 128))
        if u == 3:
            put(2, update(512 + 64 * w, 128, 128))
            put(3, update(384 + 64 * w, 128, 128))


def moved_tiles(meta, wa, wb, bases, cols):
    return pl.pallas_call(
        moved_kernel,
        grid_spec=pltpu.PrefetchScalarGridSpec(
            num_scalar_prefetch=1,
            grid=(),
            in_specs=[whole()] * 20,
            out_specs=whole(),
            scratch_shapes=[pltpu.VMEM((640, 256), F32), pltpu.VMEM((8, 8, 64, 128), F32)],
        ),
        out_shape=jax.ShapeDtypeStruct((20, 128, 128), F32),
        compiler_params=pltpu.CompilerParams(vmem_limit_bytes=32 << 20),
        cost_estimate=pl.CostEstimate(flops=10**9, bytes_accessed=6 << 20, transcendentals=0),
    )(meta, *wa, *wb, *bases, *cols)


def trailing_kernel(meta, parent_ref, moved_ref, *refs):
    a_refs, b_refs, panel_refs, out_ref = refs[0:4], refs[4:8], refs[8:16], refs[16]
    sh_ref, sl_ref, ph_ref, pl_ref = refs[17:21]
    q, g = pl.program_id(0), pl.program_id(1)
    row, col, start = meta[129], meta[130], meta[128]
    x, z = col >> 2, col & 3

    @pl.when((q == 0) & (g == 0))
    def _():
        for k in range(8):
            tile = gathered_row(meta, k)
            hi, lo = split2(panel_refs[k][...])
            ph_ref[tile >> 1, tile & 1] = hi
            pl_ref[tile >> 1, tile & 1] = lo
        for m in range(4):
            for n in range(4):
                to = ((x - m) & 3, (z - n) & 3)
                hi, lo = split2(a_refs[m][n])
                sh_ref[to[0], to[1], 0:64] = hi
                sl_ref[to[0], to[1], 0:64] = lo
                to = ((x - n) & 3, (z - m) & 3)
                hi, lo = split2(b_refs[m][n])
                sh_ref[to[0], to[1], 64:128] = hi
                sl_ref[to[0], to[1], 64:128] = lo

    def assembled(k, j):
        tile_row = 8 * (4 * g + k) + row
        tile_col = 16 * (2 * q + j) + col
        at = tile_row - meta[16 * g]
        at_col = tile_col - meta[16 * q]
        use = (at >= 0) & (at < 16) & (at_col >= 0) & (at_col < 16) & (g >= q)
        index = jnp.where(use, g * (g + 1) + (at >> 3) * (g + 1) + q, 0)
        tile = parent_ref[k, 0, j, 0] + jnp.where(use, moved_ref[index], 0.0)
        return tile, (tile_row >= tile_col) & (tile_col >= start + PANEL_T)

    first_col = 32 * q + col
    active = (32 * g + 24 + row >= first_col) & (first_col + 16 >= start + PANEL_T)

    @pl.when(active)
    def _():
        left = (sh_ref[g].reshape(512, 512), sl_ref[g].reshape(512, 512))
        right = (ph_ref[q].reshape(256, 512), pl_ref[q].reshape(256, 512))
        trailing = dot3(left, right, NT)
        for k in range(4):
            for j in range(2):
                tile, window = assembled(k, j)
                part = trailing[128 * k : 128 * k + 128, 128 * j : 128 * j + 128]
                out_ref[k, 0, j, 0] = tile - jnp.where(window, part, 0.0)

    @pl.when(jnp.logical_not(active))
    def _():
        for k in range(4):
            for j in range(2):
                out_ref[k, 0, j, 0] = assembled(k, j)[0]


def trailing_update(meta, parent_tiles, moved, sa, sb, panel):
    tiles = pl.BlockSpec((4, 1, 2, 1, 128, 128), lambda q, g, meta: (g, 0, q, 0, 0, 0))
    return pl.pallas_call(
        trailing_kernel,
        grid_spec=pltpu.PrefetchScalarGridSpec(
            num_scalar_prefetch=1,
            grid=(4, 4),
            in_specs=[tiles] + [whole()] * 17,
            out_specs=tiles,
            scratch_shapes=[pltpu.VMEM((4, 4, 128, 512), BF16)] * 2
            + [pltpu.VMEM((4, 2, 128, 512), BF16)] * 2,
        ),
        out_shape=jax.ShapeDtypeStruct(parent_tiles.shape, F32),
        compiler_params=pltpu.CompilerParams(vmem_limit_bytes=40 << 20),
        cost_estimate=pl.CostEstimate(flops=7 * 10**9, bytes_accessed=24 << 20, transcendentals=0),
    )(meta, parent_tiles, moved, *sa, *sb, *panel)


def per_device(
    contribution,
    parent_tiles,
    row_basis,
    pivot_basis,
    tile_ranks,
    block_map,
    panel_start,
    pivot_inverse,
):
    my_row = lax.axis_index("row")
    my_col = lax.axis_index("col")
    meta = jnp.concatenate(
        [block_map, tile_ranks, panel_start, jnp.stack([my_row, my_col])]
    ).astype(jnp.int32)
    shifts = [block_map[16 * u] - 32 * u for u in range(4)]
    start = panel_start[0]

    def move_row(u, *others):
        tiles = contribution[2 * u : 2 * u + 2, 0, 0 : u + 1, 0]
        return rotate(after(tiles, *others), "row", 8, shifts[u] & 7)

    def move_col(s, rows, *others):
        tiles = jnp.concatenate([rows[u][:, s] for u in range(s, 4)])
        return rotate(after(tiles, *others), "col", 16, shifts[s])

    pivots = gather_rows(pivot_basis[:, 0])
    panel_at = jnp.minimum((start + ((my_col - start) & 15)) >> 4, parent_tiles.shape[2] - 1)
    parent_panel = across_col(
        lax.dynamic_index_in_dim(parent_tiles[:, 0, :, 0], panel_at, axis=1, keepdims=False)
    )
    parts = products(meta, pivots)
    wa = scatter_sums(parts[0:4], lambda v, d: col_perm(v, 0, d), lambda v, d: col_perm(v, d, 0))
    wb = scatter_sums(parts[4:8], lambda v, d: col_perm(v, d, 0), lambda v, d: col_perm(v, 0, d))

    rows = [None] * 4
    rows[3] = move_row(3, pivots[3])
    bases = gather_rows(after(row_basis[:, 0], pivots[3]))
    rows[2] = move_row(2, parts[0])
    rows[1] = move_row(1, parts[0])
    rows[0] = move_row(0, parts[0])
    send = panel_send(meta, pivots, rows)
    got = across_col(send)
    cols = [None] * 4
    cols[3] = move_col(3, rows, send)
    cols[2] = move_col(2, rows, send)

    panel, sa, sb = panel_row(meta, bases, parent_panel, got, pivot_inverse)
    turn = []
    for r in range(8):
        for c in range(16):
            turn.append((16 * r + c, 16 * (c // 2) + 8 * (c % 2) + r))
    panel = lax.ppermute(panel, ("row", "col"), turn)
    ring_a = jnp.stack([sa] + [col_perm(sa, 0, d) for d in (1, 2, 3)])
    ring_b = jnp.stack([sb] + [col_perm(sb, d, 0) for d in (1, 2, 3)])
    panel = gather_rows(after(panel, ring_a, ring_b))
    cols[1] = move_col(1, rows, ring_a, ring_b)
    cols[0] = move_col(0, rows, ring_a, ring_b)
    sa = [ring_a] + [col_perm(ring_a, d, 0) for d in (1, 2, 3)]
    sb = [ring_b] + [col_perm(ring_b, 0, d) for d in (1, 2, 3)]
    moved = moved_tiles(meta, wa, wb, bases, cols)
    return trailing_update(meta, parent_tiles, moved, sa, sb, panel)


def solution(mesh):
    placed = (
        P(None, "row", None, "col", None, None),
        P(None, "row", None, "col", None, None),
        P(None, "row", None, None),
        P(None, "row", None, "col"),
        P(),
        P(),
        P(),
        P(),
    )
    return jax.shard_map(
        per_device,
        mesh=mesh,
        in_specs=placed,
        out_specs=P(None, "row", None, "col", None, None),
        check_vma=False,
    )
```

time: 342 us -> 317 us (0.927)
  waiting for transfers between devices: 162 us -> 116 us
  starting transfers between devices: 81.6 us -> 106 us
  blocking collectives: 18.1 us -> 0 us
  local copies, waits for them, and re-layouts: 23 us -> 35.9 us
    ppermute x24, starting transfers between devices: 36.6 us -> 61.5 us  [col_perm(): return lax.ppermute(x, 'col', pairs)]
    ppermute x12 -> x21, starting transfers between devices: 35.6 us -> 12.7 us  [row_perm(): return lax.ppermute(x, 'row', pairs)]
    ppermute x24, waiting for transfers between devices: 52.2 us -> 29.8 us  [col_perm(): return lax.ppermute(x, 'col', pairs)]
    ppermute x12 -> x21, waiting for transfers between devices: 22.7 us -> 4.56 us  [row_perm(): return lax.ppermute(x, 'row', pairs)]
    all_to_all x1 -> x0, blocking collectives: 18.1 us -> none  [per_device(): lax.all_to_all(panel_col, 'col', split_axis=0, concat_axis=0, tiled=True)]
    all_to_all x0 -> x2, starting transfers between devices: none -> 15.4 us  [across_col(): return lax.all_to_all(x, 'col', split_axis=0, concat_axis=0, tiled=True)]
    squeeze x5 -> x7, local copies, waits for them, and re-layouts: 5.09 us -> 12 us  [the longest x4 6.14 us: move_row(): tiles = contribution[2 * u:2 * u + 2, 0, 0:u + 1, 0]]
    ppermute x8 -> x7, starting transfers between devices: 8.67 us -> 14.9 us  [step(): return (lambda v: lax.ppermute(v, axis, pairs)) if k else lambda v: v]
  transfers between devices with their start and end apart: 45 -> 55, of which waited for: 21 -> 15; matrix products, arithmetic and copies ran while one was open for 8% -> 9% of each run, Pallas kernels for 4% -> 5%
where the time goes in v2:
time: 317 us; the launch traced here: 316 us
  waiting for transfers between devices  116 us (37%)
  starting transfers between devices  106 us (33%)
  local copies, waits for them, and re-layouts  35.9 us (11%)
  Pallas kernels  33.2 us (10%)
  loops' own time  10 us (3%)
  other arithmetic  9.58 us (3%)
  between operations  4.61 us (1%)
    ppermute x7, waiting for transfers between devices, step(): return (lambda v: lax.ppermute(v, axis, pairs)) if k else lambda v: v  82.1 us
    ppermute x24, starting transfers between devices, col_perm(): return lax.ppermute(x, 'col', pairs)  61.5 us
    ppermute x24, waiting for transfers between devices, col_perm(): return lax.ppermute(x, 'col', pairs)  29.8 us
    unnamed x64, local copies, waits for them, and re-layouts  16.2 us
    pallas_call x1, Pallas kernels, trailing_update(): pl.pallas_call(trailing_kernel, grid_spec=pltpu.PrefetchScalarGridSpec(nu...  16 us
    all_to_all x2, starting transfers between devices, across_col(): return lax.all_to_all(x, 'col', split_axis=0, concat_axis=0, tiled=True)  15.4 us
    ppermute x7, starting transfers between devices, step(): return (lambda v: lax.ppermute(v, axis, pairs)) if k else lambda v: v  14.9 us
    ppermute x21, starting transfers between devices, row_perm(): return lax.ppermute(x, 'row', pairs)  12.7 us
  transfers between devices with their start and end apart: 55, of which 15 were waited for; matrix products, arithmetic and copies ran while one was open for 9% of the time, Pallas kernels for 5%

profile of v2, /device:TPU:0, one launch (start us, length us, event | category | flops | bytes accessed | tf_op | source)
XLA Modules:
  0.0 315.8 jit_solution(15433550142875313504)
XLA Ops:
  7.7 8.0 %all-to-all-start = ((f32[16,128,128]{2,1,0:T(8,128)}), f32[16,128,128]{2,1,0:T(8,128)S(1)}, u32[]{:S(2)}, u32[]{:S(2)}) async-start(f32[16,128,128]{2,1,0:T(8,128)} %dynamic-slice_bitcast_fusion), calls=%async_computation | async-start | bytes 2097152 | tf_op jit(solution)/shard_map/all_to_all | solution.py:84
  25.7 16.8 %conditional.11 = (f32[2,4,128,128]{3,2,1,0:T(8,128)}) conditional(s32[]{:T(128)} %bitcast.38, f32[2,4,128,128]{3,2,1,0:T(8,128)} %slice_bitcast_fusion, f32[2,4,128,128]{3,2,1,0:T(8,128)} %slice_bitcast_fusion, f32[2,4,128,128]{3,2,1,0:T(8,128)} %slice_bitcast_fusion, ...), branch_computations={%region_24.25_spmd, %region_25.26_spmd, %region_26.27_spmd, %regio... | conditional | bytes 3145776 | solution.py:80
  27.6 14.0 %collective-permute-done.17 = f32[2,4,128,128]{3,2,1,0:T(8,128)S(1)} collective-permute-done((f32[2,4,128,128]{3,2,1,0:T(8,128)}, f32[2,4,128,128]{3,2,1,0:T(8,128)S(1)}, u32[]{:S(2)}, u32[]{:S(2)}) %collective-permute-start.17) | collective-permute-done | bytes 524320 | tf_op jit(solution)/shard_map/cond/branch_4_fun/ppermute | solution.py:78
  42.5 7.3 %shard_map.82 = (f32[4,320,128]{2,1,0:T(8,128)S(1)}, f32[4,320,128]{2,1,0:T(8,128)S(1)}, f32[4,320,128]{2,1,0:T(8,128)S(1)}, f32[4,320,128]{2,1,0:T(8,128)S(1)},...) custom-call(s32[131]{0:T(256)S(1)} %concatenate.12.meta, ...), custom_call_target="tpu_custom_call" | custom-call | flops 2000000000 | bytes 8388608 | tf_op jit(solution)/shard_map/pallas_call | solution.py:141
  56.8 11.9 %conditional.10 = (f32[2,3,128,128]{3,2,1,0:T(8,128)S(1)}) conditional(s32[]{:T(128)} %bitcast.35, f32[2,3,128,128]{3,2,1,0:T(8,128)S(1)} %slice_bitcast_fusion.1, f32[2,3,128,128]{3,2,1,0:T(8,128)S(1)} %slice_bitcast_fusion.1, f32[2,3,128,128]{3,2,1,0:T(8,128)S(1)} %slice_bitcast_fusion.1, ...), branch_computations={%region_16.17_spmd, %region_17.18_spmd, %region_18.19_spmd, %regio... | conditional | bytes 2359344 | solution.py:80
  58.7 10.0 %collective-permute-done.8 = f32[2,3,128,128]{3,2,1,0:T(8,128)S(1)} collective-permute-done((f32[2,3,128,128]{3,2,1,0:T(8,128)S(1)}, f32[2,3,128,128]{3,2,1,0:T(8,128)S(1)}, u32[]{:S(2)}, u32[]{:S(2)}) %collective-permute-start.8) | collective-permute-done | bytes 393248 | tf_op jit(solution)/shard_map/cond/branch_2_fun/ppermute | solution.py:78
  68.8 12.1 %conditional.9 = (f32[2,2,128,128]{3,2,1,0:T(8,128)}, f32[2,1,128,128]{3,2,1,0:T(8,128)}, f32[2,1,128,128]{3,2,1,0:T(8,128)}, f32[2,128,128]{2,1,0:T(8,128)}, f32[2,128,128]{2,1,0:T(8,128)}) conditional(s32[]{:T(128)} %bitcast.32, f32[2,2,128,128]{3,2,1,0:T(8,128)} %slice_bitcast_fusion.2, ...), branch_computations={%region_8.9_spmd, %region_9.10_spmd, %region_10.11_spmd, %region_1... | conditional | bytes 2621520 | solution.py:80
  69.9 6.1 %collective-permute-done.86 = f32[2,2,128,128]{3,2,1,0:T(8,128)S(1)} collective-permute-done((f32[2,2,128,128]{3,2,1,0:T(8,128)}, f32[2,2,128,128]{3,2,1,0:T(8,128)S(1)}, u32[]{:S(2)}, u32[]{:S(2)}) %collective-permute-start.86) | collective-permute-done | bytes 262176 | tf_op jit(solution)/shard_map/cond/branch_6_fun/ppermute | solution.py:78
  84.4 7.4 %all-to-all-start.1 = ((f32[16,2,128,128]{3,2,1,0:T(8,128)}), f32[16,2,128,128]{3,2,1,0:T(8,128)S(1)}, u32[]{:S(2)}, u32[]{:S(2)}) async-start(f32[16,2,128,128]{3,2,1,0:T(8,128)} %shard_map.83), calls=%async_computation.1 | async-start | bytes 4194304 | tf_op jit(solution)/shard_map/all_to_all | solution.py:84
  101.3 16.5 %conditional.15 = (f32[2,128,128]{2,1,0:T(8,128)S(1)}) conditional(s32[]{:T(128)} %bitcast.57, f32[2,128,128]{2,1,0:T(8,128)S(1)} %get-tuple-element.253, f32[2,128,128]{2,1,0:T(8,128)S(1)} %get-tuple-element.253, f32[2,128,128]{2,1,0:T(8,128)S(1)} %get-tuple-element.253, ...), branch_computations={%region_80.81_spmd, %region_81.82_spmd, %region_82.83_spmd, %regio... | conditional | bytes 786480 | solution.py:80
  104.0 13.8 %collective-permute-done.77 = f32[2,128,128]{2,1,0:T(8,128)S(1)} collective-permute-done((f32[2,128,128]{2,1,0:T(8,128)S(1)}, f32[2,128,128]{2,1,0:T(8,128)S(1)}, u32[]{:S(2)}, u32[]{:S(2)}) %collective-permute-start.77) | collective-permute-done | bytes 131104 | tf_op jit(solution)/shard_map/cond/branch_12_fun/ppermute | solution.py:78
  118.5 20.0 %conditional.14 = (f32[4,128,128]{2,1,0:T(8,128)}) conditional(s32[]{:T(128)} %bitcast.54, f32[4,128,128]{2,1,0:T(8,128)} %pad_maximum_fusion.4, f32[4,128,128]{2,1,0:T(8,128)} %pad_maximum_fusion.4, f32[4,128,128]{2,1,0:T(8,128)} %pad_maximum_fusion.4, f32[4,128,128]{2,1,0:T(8,128)} %pad_maximum_fusion.4, ...), branch_computations={%region_64.65_spmd, %region_65.66_spmd, %region_66.67_spmd, %regio... | conditional | bytes 1572912 | solution.py:80
  123.3 5.1 %collective-permute-done.60 = f32[4,128,128]{2,1,0:T(8,128)S(1)} collective-permute-done((f32[4,128,128]{2,1,0:T(8,128)}, f32[4,128,128]{2,1,0:T(8,128)S(1)}, u32[]{:S(2)}, u32[]{:S(2)}) %collective-permute-start.60) | collective-permute-done | bytes 262176 | tf_op jit(solution)/shard_map/cond/branch_10_fun/ppermute | solution.py:78
  166.5 8.7 %collective-permute-done.97 = f32[4,320,128]{2,1,0:T(8,128)} collective-permute-done((f32[4,320,128]{2,1,0:T(8,128)}, f32[4,320,128]{2,1,0:T(8,128)}, u32[]{:S(2)}, u32[]{:S(2)}) %collective-permute-start.97) | collective-permute-done | bytes 655392 | tf_op jit(solution)/shard_map/ppermute | solution.py:67
  198.5 21.5 %conditional.13 = (f32[6,128,128]{2,1,0:T(8,128)S(1)}) conditional(s32[]{:T(128)} %bitcast.51, f32[6,128,128]{2,1,0:T(8,128)S(1)} %copy-done.26, f32[6,128,128]{2,1,0:T(8,128)S(1)} %copy-done.26, f32[6,128,128]{2,1,0:T(8,128)S(1)} %copy-done.26, f32[6,128,128]{2,1,0:T(8,128)S(1)} %copy-done.26, ...), branch_computations={%region_48.49_spmd, %region_49.50_spmd, %region_50.51_spmd, %regio... | conditional | bytes 2359344 | solution.py:80
  198.9 20.9 %collective-permute-done.41 = f32[6,128,128]{2,1,0:T(8,128)S(1)} collective-permute-done((f32[6,128,128]{2,1,0:T(8,128)S(1)}, f32[6,128,128]{2,1,0:T(8,128)S(1)}, u32[]{:S(2)}, u32[]{:S(2)}) %collective-permute-start.41) | collective-permute-done | bytes 393248 | tf_op jit(solution)/shard_map/cond/branch_6_fun/ppermute | solution.py:78
  220.8 15.2 %conditional.12 = (f32[8,128,128]{2,1,0:T(8,128)}) conditional(s32[]{:T(128)} %bitcast.28, f32[8,128,128]{2,1,0:T(8,128)} %pad_maximum_fusion, f32[8,128,128]{2,1,0:T(8,128)} %pad_maximum_fusion, f32[8,128,128]{2,1,0:T(8,128)} %pad_maximum_fusion, f32[8,128,128]{2,1,0:T(8,128)} %pad_maximum_fusion, ...), branch_computations={%region_32.33_spmd, %region_33.34_spmd, %region_34.35_spmd, %regio... | conditional | bytes 3145776 | solution.py:80
  223.0 12.2 %collective-permute-done.28 = f32[8,128,128]{2,1,0:T(8,128)S(1)} collective-permute-done((f32[8,128,128]{2,1,0:T(8,128)}, f32[8,128,128]{2,1,0:T(8,128)S(1)}, u32[]{:S(2)}, u32[]{:S(2)}) %collective-permute-start.28) | collective-permute-done | bytes 524320 | tf_op jit(solution)/shard_map/cond/branch_8_fun/ppermute | solution.py:78
  236.0 9.8 %collective-permute-start.106 = (f32[320,128]{1,0:T(8,128)}, f32[320,128]{1,0:T(8,128)S(1)}, u32[]{:S(2)}, u32[]{:S(2)}) collective-permute-start(f32[320,128]{1,0:T(8,128)} %get-tuple-element.272), channel_id=1, source_target_pairs={{0,3},{1,0},{2,1},{3,2},{4,7},{5,4},{6,5},{7,6},{8,11},{9,8},{10,9... | collective-permute-start | bytes 491528 | tf_op jit(solution)/shard_map/ppermute | solution.py:67
  245.8 11.6 %collective-permute-start.105 = (f32[320,128]{1,0:T(8,128)}, f32[320,128]{1,0:T(8,128)S(1)}, u32[]{:S(2)}, u32[]{:S(2)}) collective-permute-start(f32[320,128]{1,0:T(8,128)} %get-tuple-element.273), channel_id=1, source_target_pairs={{0,2},{1,3},{2,0},{3,1},{4,6},{5,7},{6,4},{7,5},{8,10},{9,11},{10,... | collective-permute-start | bytes 491528 | tf_op jit(solution)/shard_map/ppermute | solution.py:67
  261.2 6.4 %collective-permute-start.104 = (f32[320,128]{1,0:T(8,128)}, f32[320,128]{1,0:T(8,128)S(1)}, u32[]{:S(2)}, u32[]{:S(2)}) collective-permute-start(f32[320,128]{1,0:T(8,128)} %get-tuple-element.274), channel_id=1, source_target_pairs={{0,1},{1,2},{2,3},{3,0},{4,5},{5,6},{6,7},{7,4},{8,9},{9,10},{10,1... | collective-permute-start | bytes 491528 | tf_op jit(solution)/shard_map/ppermute | solution.py:67
  280.1 8.6 %collective-permute-done.124.refs_6_ = f32[4,64,512]{2,1,0:T(8,128)S(1)} collective-permute-done((f32[4,64,512]{2,1,0:T(8,128)S(1)}, f32[4,64,512]{2,1,0:T(8,128)S(1)}, u32[]{:S(2)}, u32[]{:S(2)}) %collective-permute-start.124) | collective-permute-done | bytes 524320 | tf_op jit(solution)/shard_map/ppermute | solution.py:67
  288.7 5.1 %collective-permute-done.123.refs_5_ = f32[4,64,512]{2,1,0:T(8,128)S(1)} collective-permute-done((f32[4,64,512]{2,1,0:T(8,128)S(1)}, f32[4,64,512]{2,1,0:T(8,128)S(1)}, u32[]{:S(2)}, u32[]{:S(2)}) %collective-permute-start.123) | collective-permute-done | bytes 524320 | tf_op jit(solution)/shard_map/ppermute | solution.py:67
  299.3 16.0 %shard_map.86 = f32[16,1,8,1,128,128]{5,4,3,2,1,0:T(8,128)} custom-call(s32[131]{0:T(256)S(1)} %concatenate.12.meta, f32[16,1,8,1,128,128]{5,4,3,2,1,0:T(8,128)} %parent_ref.1, f32[20,128,128]{2,1,0:T(8,128)S(1)} %shard_map.85.moved_ref, f32[4,64,512]{2,1,0:T(8,128)S(1)} %pad_maximum_fusion.1.refs_0_, f32[4,64,512]{2,1,0:T(8,128)S(1)} %collective-permute-done.120.refs_1_, ...), custom_call_target="tpu_custom_call" | custom-call | flops 7000000000 | bytes 25165824 | tf_op jit(solution)/shard_map/pallas_call | solution.py:401
  (189 shorter events, 130.1 us)
Async XLA Ops:
  0.0 42.5 %collective-permute-start.91 = (f32[8,64,128]{2,1,0:T(8,128)}, f32[8,64,128]{2,1,0:T(8,128)S(1)}, u32[]{:S(2)}, u32[]{:S(2)}) collective-permute-start(f32[8,64,128]{2,1,0:T(8,128)} %bitcast.103), channel_id=1, source_target_pairs={{0,16},{16,0},{32,48},{48,32},{64,80},{80,64},{96,112},{112,96},{1... | collective-permute-start | bytes 786440 | tf_op jit(solution)/shard_map/ppermute | solution.py:62
  0.0 20.0 %collective-permute-start.90 = (f32[8,64,128]{2,1,0:T(8,128)}, f32[8,64,128]{2,1,0:T(8,128)S(1)}, u32[]{:S(2)}, u32[]{:S(2)}) collective-permute-start(f32[8,64,128]{2,1,0:T(8,128)} %bitcast.104), channel_id=1, source_target_pairs={{0,96},{16,112},{32,0},{48,16},{64,32},{80,48},{96,64},{112,80},{1... | collective-permute-start | bytes 786440 | tf_op jit(solution)/shard_map/ppermute | solution.py:62
  7.7 76.7 %all-to-all-start = ((f32[16,128,128]{2,1,0:T(8,128)}), f32[16,128,128]{2,1,0:T(8,128)S(1)}, u32[]{:S(2)}, u32[]{:S(2)}) async-start(f32[16,128,128]{2,1,0:T(8,128)} %dynamic-slice_bitcast_fusion), calls=%async_computation | async-start | bytes 2097152 | tf_op jit(solution)/shard_map/all_to_all | solution.py:84
  20.0 22.5 %collective-permute-start.94 = (f32[8,64,128]{2,1,0:T(8,128)S(1)}, f32[8,64,128]{2,1,0:T(8,128)S(1)}, u32[]{:S(2)}, u32[]{:S(2)}) collective-permute-start(f32[8,64,128]{2,1,0:T(8,128)S(1)} %collective-permute-done.90.refs_3_), channel_id=1, source_target_pairs={{0,16},{16,0},{32,48},{48,32},{64,80},{80,64},{96,112},{112,96},{1... | collective-permute-start | bytes 786440 | tf_op jit(solution)/shard_map/ppermute | solution.py:62
  20.1 22.4 %collective-permute-start.93 = (f32[8,64,128]{2,1,0:T(8,128)S(1)}, f32[8,64,128]{2,1,0:T(8,128)S(1)}, u32[]{:S(2)}, u32[]{:S(2)}) collective-permute-start(f32[8,64,128]{2,1,0:T(8,128)S(1)} %collective-permute-done.89.refs_2_), channel_id=1, source_target_pairs={{0,16},{16,0},{32,48},{48,32},{64,80},{80,64},{96,112},{112,96},{1... | collective-permute-start | bytes 786440 | tf_op jit(solution)/shard_map/ppermute | solution.py:62
  20.6 21.9 %collective-permute-start.92 = (f32[8,64,128]{2,1,0:T(8,128)S(1)}, f32[8,64,128]{2,1,0:T(8,128)S(1)}, u32[]{:S(2)}, u32[]{:S(2)}) collective-permute-start(f32[8,64,128]{2,1,0:T(8,128)S(1)} %collective-permute-done.88.refs_1_), channel_id=1, source_target_pairs={{0,16},{16,0},{32,48},{48,32},{64,80},{80,64},{96,112},{112,96},{1... | collective-permute-start | bytes 786440 | tf_op jit(solution)/shard_map/ppermute | solution.py:62
  84.4 73.8 %all-to-all-start.1 = ((f32[16,2,128,128]{3,2,1,0:T(8,128)}), f32[16,2,128,128]{3,2,1,0:T(8,128)S(1)}, u32[]{:S(2)}, u32[]{:S(2)}) async-start(f32[16,2,128,128]{3,2,1,0:T(8,128)} %shard_map.83), calls=%async_computation.1 | async-start | bytes 4194304 | tf_op jit(solution)/shard_map/all_to_all | solution.py:84
  91.8 46.8 %collective-permute-start.109 = (f32[8,64,128]{2,1,0:T(8,128)S(1)}, f32[8,64,128]{2,1,0:T(8,128)}, u32[]{:S(2)}, u32[]{:S(2)}) collective-permute-start(f32[8,64,128]{2,1,0:T(8,128)S(1)} %bitcast.97), channel_id=1, source_target_pairs={{0,96},{16,112},{32,0},{48,16},{64,32},{80,48},{96,64},{112,80},{1... | collective-permute-start | bytes 786440 | tf_op jit(solution)/shard_map/ppermute | solution.py:62
  94.2 44.9 %collective-permute-start.108 = (f32[8,64,128]{2,1,0:T(8,128)S(1)}, f32[8,64,128]{2,1,0:T(8,128)}, u32[]{:S(2)}, u32[]{:S(2)}) collective-permute-start(f32[8,64,128]{2,1,0:T(8,128)S(1)} %bitcast.98), channel_id=1, source_target_pairs={{0,64},{16,80},{32,96},{48,112},{64,0},{80,16},{96,32},{112,48},{1... | collective-permute-start | bytes 786440 | tf_op jit(solution)/shard_map/ppermute | solution.py:62
  94.6 44.5 %collective-permute-start.107 = (f32[8,64,128]{2,1,0:T(8,128)S(1)}, f32[8,64,128]{2,1,0:T(8,128)}, u32[]{:S(2)}, u32[]{:S(2)}) collective-permute-start(f32[8,64,128]{2,1,0:T(8,128)S(1)} %bitcast.99), channel_id=1, source_target_pairs={{0,32},{16,48},{32,64},{48,80},{64,96},{80,112},{96,0},{112,16},{1... | collective-permute-start | bytes 786440 | tf_op jit(solution)/shard_map/ppermute | solution.py:62
  96.9 55.0 %collective-permute-start.95 = (f32[4,320,128]{2,1,0:T(8,128)}, f32[4,320,128]{2,1,0:T(8,128)}, u32[]{:S(2)}, u32[]{:S(2)}) collective-permute-start(f32[4,320,128]{2,1,0:T(8,128)} %copy-done.24), channel_id=1, source_target_pairs={{0,1},{1,2},{2,3},{3,0},{4,5},{5,6},{6,7},{7,4},{8,9},{9,10},{10,1... | collective-permute-start | bytes 1966088 | tf_op jit(solution)/shard_map/ppermute | solution.py:67
  140.8 25.6 %collective-permute-start.96 = (f32[4,320,128]{2,1,0:T(8,128)}, f32[4,320,128]{2,1,0:T(8,128)}, u32[]{:S(2)}, u32[]{:S(2)}) collective-permute-start(f32[4,320,128]{2,1,0:T(8,128)} %copy-done.23), channel_id=1, source_target_pairs={{0,2},{1,3},{2,0},{3,1},{4,6},{5,7},{6,4},{7,5},{8,10},{9,11},{10,... | collective-permute-start | bytes 1966088 | tf_op jit(solution)/shard_map/ppermute | solution.py:67
  145.4 29.8 %collective-permute-start.97 = (f32[4,320,128]{2,1,0:T(8,128)}, f32[4,320,128]{2,1,0:T(8,128)}, u32[]{:S(2)}, u32[]{:S(2)}) collective-permute-start(f32[4,320,128]{2,1,0:T(8,128)} %copy-done.22), channel_id=1, source_target_pairs={{0,3},{1,0},{2,1},{3,2},{4,7},{5,4},{6,5},{7,6},{8,11},{9,8},{10,9... | collective-permute-start | bytes 1966088 | tf_op jit(solution)/shard_map/ppermute | solution.py:67
  146.1 32.2 %collective-permute-start.101 = (f32[4,320,128]{2,1,0:T(8,128)}, f32[4,320,128]{2,1,0:T(8,128)}, u32[]{:S(2)}, u32[]{:S(2)}) collective-permute-start(f32[4,320,128]{2,1,0:T(8,128)} %copy-done.21), channel_id=1, source_target_pairs={{0,4},{1,5},{2,6},{3,7},{4,8},{5,9},{6,10},{7,11},{8,12},{9,13},{1... | collective-permute-start | bytes 1966088 | tf_op jit(solution)/shard_map/ppermute | solution.py:67
  149.5 30.9 %collective-permute-start.102 = (f32[4,320,128]{2,1,0:T(8,128)}, f32[4,320,128]{2,1,0:T(8,128)}, u32[]{:S(2)}, u32[]{:S(2)}) collective-permute-start(f32[4,320,128]{2,1,0:T(8,128)} %copy-done.20), channel_id=1, source_target_pairs={{0,8},{1,9},{2,10},{3,11},{4,12},{5,13},{6,14},{7,15},{8,0},{9,1},... | collective-permute-start | bytes 1966088 | tf_op jit(solution)/shard_map/ppermute | solution.py:67
  152.0 30.5 %collective-permute-start.103 = (f32[4,320,128]{2,1,0:T(8,128)}, f32[4,320,128]{2,1,0:T(8,128)}, u32[]{:S(2)}, u32[]{:S(2)}) collective-permute-start(f32[4,320,128]{2,1,0:T(8,128)} %copy-done.19), channel_id=1, source_target_pairs={{0,12},{1,13},{2,14},{3,15},{4,0},{5,1},{6,2},{7,3},{8,4},{9,5},{1... | collective-permute-start | bytes 1966088 | tf_op jit(solution)/shard_map/ppermute | solution.py:67
  187.3 70.1 %collective-permute-start.100 = (f32[320,128]{1,0:T(8,128)}, f32[320,128]{1,0:T(8,128)S(1)}, u32[]{:S(2)}, u32[]{:S(2)}) collective-permute-start(f32[320,128]{1,0:T(8,128)} %get-tuple-element.276), channel_id=1, source_target_pairs={{0,12},{1,13},{2,14},{3,15},{4,0},{5,1},{6,2},{7,3},{8,4},{9,5},{1... | collective-permute-start | bytes 491528 | tf_op jit(solution)/shard_map/ppermute | solution.py:67
  190.6 55.2 %collective-permute-start.126 = (f32[128,512]{1,0:T(8,128)}, f32[128,512]{1,0:T(8,128)S(1)}, u32[]{:S(2)}, u32[]{:S(2)}) collective-permute-start(f32[128,512]{1,0:T(8,128)} %get-tuple-element.254), channel_id=1, source_target_pairs={{0,0},{1,8},{2,16},{3,24},{4,32},{5,40},{6,48},{7,56},{8,64},{9,72... | collective-permute-start | bytes 786440 | tf_op jit(solution)/shard_map/ppermute | solution.py:469
  192.2 65.8 %collective-permute-start.99 = (f32[320,128]{1,0:T(8,128)}, f32[320,128]{1,0:T(8,128)S(1)}, u32[]{:S(2)}, u32[]{:S(2)}) collective-permute-start(f32[320,128]{1,0:T(8,128)} %get-tuple-element.277), channel_id=1, source_target_pairs={{0,8},{1,9},{2,10},{3,11},{4,12},{5,13},{6,14},{7,15},{8,0},{9,1},... | collective-permute-start | bytes 491528 | tf_op jit(solution)/shard_map/ppermute | solution.py:67
  197.2 60.9 %collective-permute-start.98 = (f32[320,128]{1,0:T(8,128)}, f32[320,128]{1,0:T(8,128)S(1)}, u32[]{:S(2)}, u32[]{:S(2)}) collective-permute-start(f32[320,128]{1,0:T(8,128)} %get-tuple-element.278), channel_id=1, source_target_pairs={{0,4},{1,5},{2,6},{3,7},{4,8},{5,9},{6,10},{7,11},{8,12},{9,13},{1... | collective-permute-start | bytes 491528 | tf_op jit(solution)/shard_map/ppermute | solution.py:67
  198.5 21.2 %collective-permute-start.41 = (f32[6,128,128]{2,1,0:T(8,128)S(1)}, f32[6,128,128]{2,1,0:T(8,128)S(1)}, u32[]{:S(2)}, u32[]{:S(2)}) collective-permute-start(f32[6,128,128]{2,1,0:T(8,128)S(1)} %param.54), channel_id=1, source_target_pairs={{0,6},{1,7},{2,8},{3,9},{4,10},{5,11},{6,12},{7,13},{8,14},{9,15},... | collective-permute-start | bytes 1179656 | tf_op jit(solution)/shard_map/cond/branch_6_fun/ppermute | solution.py:78
  236.0 22.2 %collective-permute-start.106 = (f32[320,128]{1,0:T(8,128)}, f32[320,128]{1,0:T(8,128)S(1)}, u32[]{:S(2)}, u32[]{:S(2)}) collective-permute-start(f32[320,128]{1,0:T(8,128)} %get-tuple-element.272), channel_id=1, source_target_pairs={{0,3},{1,0},{2,1},{3,2},{4,7},{5,4},{6,5},{7,6},{8,11},{9,8},{10,9... | collective-permute-start | bytes 491528 | tf_op jit(solution)/shard_map/ppermute | solution.py:67
  257.4 22.7 %collective-permute-start.125 = (f32[4,64,512]{2,1,0:T(8,128)S(1)}, f32[4,64,512]{2,1,0:T(8,128)S(1)}, u32[]{:S(2)}, u32[]{:S(2)}) collective-permute-start(f32[4,64,512]{2,1,0:T(8,128)S(1)} %pad_maximum_fusion.2.refs_4_), channel_id=1, source_target_pairs={{0,3},{1,0},{2,1},{3,2},{4,7},{5,4},{6,5},{7,6},{8,11},{9,8},{10,9... | collective-permute-start | bytes 1572872 | tf_op jit(solution)/shard_map/ppermute | solution.py:67
  280.1 19.2 %collective-permute-start.120 = (f32[4,64,512]{2,1,0:T(8,128)S(1)}, f32[4,64,512]{2,1,0:T(8,128)S(1)}, u32[]{:S(2)}, u32[]{:S(2)}) collective-permute-start(f32[4,64,512]{2,1,0:T(8,128)S(1)} %pad_maximum_fusion.1.refs_0_), channel_id=1, source_target_pairs={{0,4},{1,5},{2,6},{3,7},{4,8},{5,9},{6,10},{7,11},{8,12},{9,13},{1... | collective-permute-start | bytes 1572872 | tf_op jit(solution)/shard_map/ppermute | solution.py:67
  (63 other events, 848.0 us)
